TPU v7x, 256 devices: a whole 4x4x8 slice. The times are simulated.
256 devices in a mesh: gz: 16 (over y_lo, x, core), gy: 16 (over z, y_hi).
Axes of the slice: x: 4, y: 4 (y_hi: 2, y_lo: 2; y = y_hi * 2 + y_lo), z: 8, core: 2. Of those that a mesh axis runs over, the one named last changes fastest.
Arguments:
- electric: float32 [3, 256, 128, 256], P(None, 'gz', 'gy'), may hold values from -6 to 6
- magnetic: float32 [3, 256, 128, 256], P(None, 'gz', 'gy'), may hold values from -6 to 6
- material: int32 [256, 128, 256], P('gz', 'gy'), may hold values from 0 to 15
- incoming: int32 [32, 128, 256], P(None, 'gy'), may hold values from 0 to 15
- shift_flags: int32 [8], replicated, may hold values from 0 to 1, as said below
- eps_table: float32 [16], replicated, may hold values from 1 to 6
- sigma_table: float32 [16], replicated, may hold values from 0 to 1
- kerr_table: float32 [16], replicated, may hold values from 0.05 to 0.5
Outputs:
- electric_out: float32 [3, 256, 128, 256], P(None, 'gz', 'gy')
- magnetic_out: float32 [3, 256, 128, 256], P(None, 'gz', 'gy')
Inputs may be any that keep to these rules, and one draw needn't show every extreme that they name: `shift_flags`: exactly 4 entries are 1, the others 0.
All inputs are finite; a program needn't handle non-finite values.
Results may differ from a plain program's by a relative error of at most 0.00002.
Values sent between devices are 32-bit elements; how exact they have to be, the bound alone decides.
A program may use at most 64 MiB of HBM per device.

v0:
```python
import jax
import jax.numpy as jnp
from jax import lax
from jax.sharding import PartitionSpec as P

STEPS = 8
SHIFT = 8


courant_number = 0.5


def from_behind(value, axis, steps):
    count = lax.axis_size(axis)
    leading, last = (max(0, -steps), min(count, count - steps))
    return lax.ppermute(value, axis, [(source, source + steps) for source in range(leading, last)])


def forward_face(field, face, axis_no):
    length = field.shape[axis_no]
    shifted = jnp.concatenate(
        [lax.slice_in_dim(field, 1, length, axis=axis_no), face], axis=axis_no
    )
    return shifted - field


def backward_face(field, face, axis_no):
    length = field.shape[axis_no]
    shifted = jnp.concatenate(
        [face, lax.slice_in_dim(field, 0, length - 1, axis=axis_no)], axis=axis_no
    )
    return field - shifted


def forward_zero(field, axis_no):
    length = field.shape[axis_no]
    shifted = jnp.concatenate(
        [
            lax.slice_in_dim(field, 1, length, axis=axis_no),
            jnp.zeros_like(lax.slice_in_dim(field, 0, 1, axis=axis_no)),
        ],
        axis=axis_no,
    )
    return shifted - field


def backward_zero(field, axis_no):
    length = field.shape[axis_no]
    shifted = jnp.concatenate(
        [
            jnp.zeros_like(lax.slice_in_dim(field, 0, 1, axis=axis_no)),
            lax.slice_in_dim(field, 0, length - 1, axis=axis_no),
        ],
        axis=axis_no,
    )
    return field - shifted


def curl_faces(vector, face_z, face_y, with_face, with_zero):

    def derivative(component, axis_no):
        if axis_no == 0:
            return with_face(vector[component], face_z[component], 0)
        if axis_no == 1:
            return with_face(vector[component], face_y[component], 1)
        return with_zero(vector[component], 2)

    part_x = derivative(2, 1) - derivative(1, 0)
    part_y = derivative(0, 0) - derivative(2, 2)
    part_z = derivative(1, 2) - derivative(0, 1)
    return jnp.stack([part_x, part_y, part_z])


def e_update(electric, curl_h, coefs):
    square = electric[0] * electric[0] + electric[1] * electric[1] + electric[2] * electric[2]
    permit = coefs[0] + coefs[2] * square
    damping = 0.5 * coefs[1] / permit
    return ((1.0 - damping) * electric + courant_number / permit * curl_h) / (1.0 + damping)


def lookup(id_map, eps_table, sigma_table, kerr_table):
    results = []
    for tables in (eps_table, sigma_table, kerr_table):
        summed = jnp.zeros(id_map.shape, jnp.float32)
        for entry_no in range(tables.shape[0]):
            summed = summed + jnp.where(id_map == entry_no, tables[entry_no], jnp.float32(0.0))
        results.append(summed)
    return jnp.stack(results)


def body(electric, magnetic, material, incoming, shift_flags, eps_table, sigma_table, kerr_table):
    coefs = lookup(material, eps_table, sigma_table, kerr_table)
    is_last = lax.axis_index("gz") == lax.axis_size("gz") - 1
    done_count = jnp.int32(0)
    for step_no in range(STEPS):
        shift_on = shift_flags[step_no] == 1
        new_ids = lax.dynamic_slice_in_dim(incoming, done_count * SHIFT, SHIFT, 0)
        new_coefs = lookup(new_ids, eps_table, sigma_table, kerr_table)
        stacked = jnp.concatenate([electric, magnetic, coefs], 0)
        moved_part = from_behind(stacked[:, :SHIFT], "gz", -1)
        entering = jnp.concatenate(
            [moved_part[:6], jnp.where(is_last, new_coefs, moved_part[6:])], 0
        )
        moved = jnp.concatenate([stacked[:, SHIFT:], entering], 1)
        stacked = jnp.where(shift_on, moved, stacked)
        electric, magnetic, coefs = (stacked[0:3], stacked[3:6], stacked[6:9])
        done_count = done_count + shift_flags[step_no]
        upper_z = from_behind(electric[:, 0:1], "gz", -1)
        upper_y = from_behind(electric[:, :, 0:1], "gy", -1)
        magnetic = magnetic - courant_number * curl_faces(
            electric, upper_z, upper_y, forward_face, forward_zero
        )
        lower_z = from_behind(magnetic[:, -1:], "gz", 1)
        lower_y = from_behind(magnetic[:, :, -1:], "gy", 1)
        curl_h = curl_faces(magnetic, lower_z, lower_y, backward_face, backward_zero)
        electric = e_update(electric, curl_h, coefs)
    return (electric, magnetic)


def solution(mesh):
    return jax.shard_map(
        body,
        mesh=mesh,
        in_specs=(
            P(None, "gz", "gy", None),
            P(None, "gz", "gy", None),
            P("gz", "gy", None),
            P(None, "gy", None),
            P(),
            P(),
            P(),
            P(),
        ),
        out_specs=(P(None, "gz", "gy", None), P(None, "gz", "gy", None)),
        check_vma=False,
    )
```

profile of v0, /device:TPU:119, one launch (start us, length us, event | category | flops | bytes accessed | tf_op | source)
XLA Modules:
  0.0 475.0 jit_solution(6836828577268234593)
XLA Ops:
  8.6 10.6 %bitcast_dynamic-update-slice_fusion.2 = (f32[9,16,8,256]{3,2,1,0:T(8,128)S(1)}, pred[16,8,256]{2,1,0:T(8,128)(4,1)S(1)}, pred[16,8,256]{2,1,0:T(8,128)(4,1)S(1)...) fusion(f32[9,16,8,256]{3,2,1,0:T(8,128)S(1)} %constant_dynamic-, ...), kind=kLoop, calls=%fused_computation.273 | loop fusion | flops 1540096 | bytes 786496
  19.2 10.2 %bitcast_dynamic-update-slice_fusion.1 = f32[9,16,8,256]{3,2,1,0:T(8,128)S(1)} fusion(f32[9,16,8,256]{3,2,1,0:T(8,128)S(1)} %get-tuple-element.154, pred[16,8,256]{2,1,0:T(8,128)(4,1)S(1)} %get-tuple-element.170, pred[16,8,256]{2,1,0:T(8,128)(4,1)S(1)} %get-tuple-element.169, pred[16,8,256]{2,1,0:T(8,128)(4,1)S(1)} %get-tuple-element.168, ...), kind=kLoop, calls=%fused_computation.272 | loop fusion | flops 1015808 | bytes 655424
  29.4 10.2 %bitcast_dynamic-update-slice_fusion = f32[9,16,8,256]{3,2,1,0:T(8,128)S(1)} fusion(f32[9,16,8,256]{3,2,1,0:T(8,128)S(1)} %bitcast_dynamic-update-slice_fusion.1, pred[16,8,256]{2,1,0:T(8,128)(4,1)S(1)} %get-tuple-element.170, pred[16,8,256]{2,1,0:T(8,128)(4,1)S(1)} %get-tuple-element.169, pred[16,8,256]{2,1,0:T(8,128)(4,1)S(1)} %get-tuple-element.168, ...), kind=kLoop, calls=%fused_computation.271 | loop fusion | flops 1015808 | bytes 655424 | tf_op jit(solution)/shard_map/concatenate | solution.py:99
  39.7 2.6 collective-permute-start
  45.9 11.2 %add_bitcast_fusion.19 = (f32[1,8,8,256]{3,2,1,0:T(8,128)S(1)}, pred[8,8,256]{2,1,0:T(8,128)(4,1)}, pred[8,8,256]{2,1,0:T(8,128)(4,1)}, pred[8,8,256]{2,1,0:T(8,...) fusion(f32[]{:T(128)} %bitcast.23, f32[]{:T(128)} %bitcast.22, ...), kind=kLoop, calls=%fused_computation.365 | loop fusion | flops 1540096 | bytes 786500 | tf_op jit(solution)/shard_map/stack | solution.py:88
  57.1 10.1 %add_bitcast_fusion.30 = f32[1,8,8,256]{3,2,1,0:T(8,128)S(1)} fusion(pred[8,8,256]{2,1,0:T(8,128)(4,1)S(1)} %get-tuple-element.381, pred[8,8,256]{2,1,0:T(8,128)(4,1)S(1)} %get-tuple-element.382, pred[8,8,256]{2,1,0:T(8,128)(4,1)S(1)} %get-tuple-element.383, pred[8,8,256]{2,1,0:T(8,128)(4,1)S(1)} %get-tuple-element.384, ...), kind=kLoop, calls=%fused_computation.376 | loop fusion | flops 507904 | bytes 327744 | tf_op jit(solution)/shard_map/stack | solution.py:88
  67.1 10.1 %add_bitcast_fusion.29 = f32[1,8,8,256]{3,2,1,0:T(8,128)S(1)} fusion(pred[8,8,256]{2,1,0:T(8,128)(4,1)S(1)} %get-tuple-element.381, pred[8,8,256]{2,1,0:T(8,128)(4,1)S(1)} %get-tuple-element.382, pred[8,8,256]{2,1,0:T(8,128)(4,1)S(1)} %get-tuple-element.383, pred[8,8,256]{2,1,0:T(8,128)(4,1)S(1)} %get-tuple-element.384, ...), kind=kLoop, calls=%fused_computation.375 | loop fusion | flops 507904 | bytes 327744 | tf_op jit(solution)/shard_map/stack | solution.py:88
  81.9 3.0 collective-permute-done.2
  84.9 3.5 collective-permute-done.1
  88.8 6.6 %collective-permute-start.4 = (f32[3,1,8,256]{3,2,1,0:T(8,128)S(1)}, f32[3,1,8,256]{3,2,1,0:T(8,128)S(1)}, u32[]{:S(2)}, u32[]{:S(2)}) collective-permute-start(f32[3,1,8,256]{3,2,1,0:T(8,128)S(1)} %slice.2193), channel_id=1, source_target_pairs={{0,16},{16,32},{32,48},{48,64},{64,80},{80,96},{96,112},{112,128},... | collective-permute-start | bytes 73736 | tf_op jit(solution)/shard_map/ppermute | solution.py:16
  95.6 2.4 collective-permute-start.3
  98.0 3.9 collective-permute-done.3
  107.4 11.2 %add_bitcast_fusion.10 = (f32[1,8,8,256]{3,2,1,0:T(8,128)S(1)}, pred[8,8,256]{2,1,0:T(8,128)(4,1)S(1)}, pred[8,8,256]{2,1,0:T(8,128)(4,1)S(1)}, pred[8,8,256]{2,...) fusion(f32[]{:T(128)} %bitcast.23, f32[]{:T(128)} %bitcast.22, ...), kind=kLoop, calls=%fused_computation.356 | loop fusion | flops 1540096 | bytes 786504 | tf_op jit(solution)/shard_map/stack | solution.py:88
  118.6 10.1 %add_bitcast_fusion.26 = f32[1,8,8,256]{3,2,1,0:T(8,128)S(1)} fusion(pred[8,8,256]{2,1,0:T(8,128)(4,1)S(1)} %get-tuple-element.330, pred[8,8,256]{2,1,0:T(8,128)(4,1)S(1)} %get-tuple-element.331, pred[8,8,256]{2,1,0:T(8,128)(4,1)S(1)} %get-tuple-element.332, pred[8,8,256]{2,1,0:T(8,128)(4,1)S(1)} %get-tuple-element.333, ...), kind=kLoop, calls=%fused_computation.372 | loop fusion | flops 507904 | bytes 327744 | tf_op jit(solution)/shard_map/stack | solution.py:88
  128.7 10.1 %add_bitcast_fusion.27 = f32[1,8,8,256]{3,2,1,0:T(8,128)S(1)} fusion(pred[8,8,256]{2,1,0:T(8,128)(4,1)S(1)} %get-tuple-element.330, pred[8,8,256]{2,1,0:T(8,128)(4,1)S(1)} %get-tuple-element.331, pred[8,8,256]{2,1,0:T(8,128)(4,1)S(1)} %get-tuple-element.332, pred[8,8,256]{2,1,0:T(8,128)(4,1)S(1)} %get-tuple-element.333, ...), kind=kLoop, calls=%fused_computation.373 | loop fusion | flops 507904 | bytes 327744 | tf_op jit(solution)/shard_map/stack | solution.py:88
  143.2 3.2 collective-permute-done.7
  146.4 3.3 collective-permute-done.6
  150.1 7.0 %collective-permute-start.9 = (f32[3,1,8,256]{3,2,1,0:T(8,128)S(1)}, f32[3,1,8,256]{3,2,1,0:T(8,128)S(1)}, u32[]{:S(2)}, u32[]{:S(2)}) collective-permute-start(f32[3,1,8,256]{3,2,1,0:T(8,128)S(1)} %slice.2233), channel_id=1, source_target_pairs={{0,16},{16,32},{32,48},{48,64},{64,80},{80,96},{96,112},{112,128},... | collective-permute-start | bytes 73736 | tf_op jit(solution)/shard_map/ppermute | solution.py:16
  157.2 2.4 collective-permute-start.8
  159.6 3.9 collective-permute-done.8
  166.6 11.2 %add_bitcast_fusion.13 = (f32[1,8,8,256]{3,2,1,0:T(8,128)S(1)}, pred[8,8,256]{2,1,0:T(8,128)(4,1)}, pred[8,8,256]{2,1,0:T(8,128)(4,1)}, pred[8,8,256]{2,1,0:T(8,...) fusion(f32[]{:T(128)} %bitcast.23, f32[]{:T(128)} %bitcast.22, ...), kind=kLoop, calls=%fused_computation.359 | loop fusion | flops 1540096 | bytes 786504 | tf_op jit(solution)/shard_map/stack | solution.py:88
  177.8 10.1 %add_bitcast_fusion.23 = f32[1,8,8,256]{3,2,1,0:T(8,128)S(1)} fusion(pred[8,8,256]{2,1,0:T(8,128)(4,1)S(1)} %get-tuple-element.347, pred[8,8,256]{2,1,0:T(8,128)(4,1)S(1)} %get-tuple-element.348, pred[8,8,256]{2,1,0:T(8,128)(4,1)S(1)} %get-tuple-element.349, pred[8,8,256]{2,1,0:T(8,128)(4,1)S(1)} %get-tuple-element.350, ...), kind=kLoop, calls=%fused_computation.369 | loop fusion | flops 507904 | bytes 327744 | tf_op jit(solution)/shard_map/stack | solution.py:88
  187.9 10.1 %add_bitcast_fusion.24 = f32[1,8,8,256]{3,2,1,0:T(8,128)S(1)} fusion(pred[8,8,256]{2,1,0:T(8,128)(4,1)S(1)} %get-tuple-element.347, pred[8,8,256]{2,1,0:T(8,128)(4,1)S(1)} %get-tuple-element.348, pred[8,8,256]{2,1,0:T(8,128)(4,1)S(1)} %get-tuple-element.349, pred[8,8,256]{2,1,0:T(8,128)(4,1)S(1)} %get-tuple-element.350, ...), kind=kLoop, calls=%fused_computation.370 | loop fusion | flops 507904 | bytes 327744 | tf_op jit(solution)/shard_map/stack | solution.py:88
  202.3 3.5 collective-permute-done.12
  205.9 3.0 collective-permute-done.11
  209.3 7.0 %collective-permute-start.14 = (f32[3,1,8,256]{3,2,1,0:T(8,128)S(1)}, f32[3,1,8,256]{3,2,1,0:T(8,128)S(1)}, u32[]{:S(2)}, u32[]{:S(2)}) collective-permute-start(f32[3,1,8,256]{3,2,1,0:T(8,128)S(1)} %slice.2273), channel_id=1, source_target_pairs={{0,16},{16,32},{32,48},{48,64},{64,80},{80,96},{96,112},{112,128},... | collective-permute-start | bytes 73736 | tf_op jit(solution)/shard_map/ppermute | solution.py:16
  216.3 2.4 collective-permute-start.13
  218.8 3.9 collective-permute-done.13
  226.0 10.6 %add_bitcast_fusion.16 = (f32[1,8,8,256]{3,2,1,0:T(8,128)S(1)}, pred[8,8,256]{2,1,0:T(8,128)(4,1)S(1)}, pred[8,8,256]{2,1,0:T(8,128)(4,1)S(1)}, pred[8,8,256]{2,...) fusion(f32[]{:T(128)} %bitcast.23, f32[]{:T(128)} %bitcast.22, ...), kind=kLoop, calls=%fused_computation.362 | loop fusion | flops 1540096 | bytes 786504 | tf_op jit(solution)/shard_map/stack | solution.py:88
  236.6 10.1 %add_bitcast_fusion.20 = f32[1,8,8,256]{3,2,1,0:T(8,128)S(1)} fusion(pred[8,8,256]{2,1,0:T(8,128)(4,1)S(1)} %get-tuple-element.364, pred[8,8,256]{2,1,0:T(8,128)(4,1)S(1)} %get-tuple-element.365, pred[8,8,256]{2,1,0:T(8,128)(4,1)S(1)} %get-tuple-element.366, pred[8,8,256]{2,1,0:T(8,128)(4,1)S(1)} %get-tuple-element.367, ...), kind=kLoop, calls=%fused_computation.366 | loop fusion | flops 507904 | bytes 327744 | tf_op jit(solution)/shard_map/stack | solution.py:88
  246.7 10.1 %add_bitcast_fusion.21 = f32[1,8,8,256]{3,2,1,0:T(8,128)S(1)} fusion(pred[8,8,256]{2,1,0:T(8,128)(4,1)S(1)} %get-tuple-element.364, pred[8,8,256]{2,1,0:T(8,128)(4,1)S(1)} %get-tuple-element.365, pred[8,8,256]{2,1,0:T(8,128)(4,1)S(1)} %get-tuple-element.366, pred[8,8,256]{2,1,0:T(8,128)(4,1)S(1)} %get-tuple-element.367, ...), kind=kLoop, calls=%fused_computation.367 | loop fusion | flops 507904 | bytes 327744 | tf_op jit(solution)/shard_map/stack | solution.py:88
  261.1 3.5 collective-permute-done.17
  264.7 3.0 collective-permute-done.16
  268.1 7.0 %collective-permute-start.19 = (f32[3,1,8,256]{3,2,1,0:T(8,128)S(1)}, f32[3,1,8,256]{3,2,1,0:T(8,128)S(1)}, u32[]{:S(2)}, u32[]{:S(2)}) collective-permute-start(f32[3,1,8,256]{3,2,1,0:T(8,128)S(1)} %slice.2313), channel_id=1, source_target_pairs={{0,16},{16,32},{32,48},{48,64},{64,80},{80,96},{96,112},{112,128},... | collective-permute-start | bytes 73736 | tf_op jit(solution)/shard_map/ppermute | solution.py:16
  275.1 2.4 collective-permute-start.18
  277.6 3.9 collective-permute-done.18
  284.9 10.1 %add_bitcast_fusion.17 = f32[1,8,8,256]{3,2,1,0:T(8,128)S(1)} fusion(pred[8,8,256]{2,1,0:T(8,128)(4,1)S(1)} %copy-done.24, pred[8,8,256]{2,1,0:T(8,128)(4,1)S(1)} %copy-done.23, pred[8,8,256]{2,1,0:T(8,128)(4,1)S(1)} %copy-done.22, pred[8,8,256]{2,1,0:T(8,128)(4,1)S(1)} %copy-done.21, pred[8,8,256]{2,1,0:T(8,128)(4,1)S(1)} %copy-done.20, ...), kind=kLoop, calls=%fused_computation.363 | loop fusion | flops 507904 | bytes 327744 | tf_op jit(solution)/shard_map/stack | solution.py:88
  295.0 10.1 %add_bitcast_fusion.18 = f32[1,8,8,256]{3,2,1,0:T(8,128)S(1)} fusion(pred[8,8,256]{2,1,0:T(8,128)(4,1)S(1)} %copy-done.24, pred[8,8,256]{2,1,0:T(8,128)(4,1)S(1)} %copy-done.23, pred[8,8,256]{2,1,0:T(8,128)(4,1)S(1)} %copy-done.22, pred[8,8,256]{2,1,0:T(8,128)(4,1)S(1)} %copy-done.21, pred[8,8,256]{2,1,0:T(8,128)(4,1)S(1)} %copy-done.20, ...), kind=kLoop, calls=%fused_computation.364 | loop fusion | flops 507904 | bytes 327744 | tf_op jit(solution)/shard_map/stack | solution.py:88
  309.4 3.5 collective-permute-done.22
  312.9 3.0 collective-permute-done.21
  316.3 7.0 %collective-permute-start.24 = (f32[3,1,8,256]{3,2,1,0:T(8,128)S(1)}, f32[3,1,8,256]{3,2,1,0:T(8,128)S(1)}, u32[]{:S(2)}, u32[]{:S(2)}) collective-permute-start(f32[3,1,8,256]{3,2,1,0:T(8,128)S(1)} %slice.2353), channel_id=1, source_target_pairs={{0,16},{16,32},{32,48},{48,64},{64,80},{80,96},{96,112},{112,128},... | collective-permute-start | bytes 73736 | tf_op jit(solution)/shard_map/ppermute | solution.py:16
  323.4 2.4 collective-permute-start.23
  325.8 3.9 collective-permute-done.23
  332.9 10.1 %add_bitcast_fusion.14 = f32[1,8,8,256]{3,2,1,0:T(8,128)S(1)} fusion(pred[8,8,256]{2,1,0:T(8,128)(4,1)S(1)} %get-tuple-element.58, pred[8,8,256]{2,1,0:T(8,128)(4,1)S(1)} %get-tuple-element.57, pred[8,8,256]{2,1,0:T(8,128)(4,1)S(1)} %get-tuple-element.56, pred[8,8,256]{2,1,0:T(8,128)(4,1)S(1)} %get-tuple-element.55, ...), kind=kLoop, calls=%fused_computation.360 | loop fusion | flops 507904 | bytes 327744 | tf_op jit(solution)/shard_map/stack | solution.py:88
  342.9 10.1 %add_bitcast_fusion.15 = f32[1,8,8,256]{3,2,1,0:T(8,128)S(1)} fusion(pred[8,8,256]{2,1,0:T(8,128)(4,1)S(1)} %get-tuple-element.58, pred[8,8,256]{2,1,0:T(8,128)(4,1)S(1)} %get-tuple-element.57, pred[8,8,256]{2,1,0:T(8,128)(4,1)S(1)} %get-tuple-element.56, pred[8,8,256]{2,1,0:T(8,128)(4,1)S(1)} %get-tuple-element.55, ...), kind=kLoop, calls=%fused_computation.361 | loop fusion | flops 507904 | bytes 327744 | tf_op jit(solution)/shard_map/stack | solution.py:88
  357.4 3.5 collective-permute-done.27
  360.9 3.0 collective-permute-done.26
  364.3 7.0 %collective-permute-start.29 = (f32[3,1,8,256]{3,2,1,0:T(8,128)S(1)}, f32[3,1,8,256]{3,2,1,0:T(8,128)S(1)}, u32[]{:S(2)}, u32[]{:S(2)}) collective-permute-start(f32[3,1,8,256]{3,2,1,0:T(8,128)S(1)} %slice.2393), channel_id=1, source_target_pairs={{0,16},{16,32},{32,48},{48,64},{64,80},{80,96},{96,112},{112,128},... | collective-permute-start | bytes 73736 | tf_op jit(solution)/shard_map/ppermute | solution.py:16
  371.4 2.4 collective-permute-start.28
  373.8 3.9 collective-permute-done.28
  381.1 10.1 %add_bitcast_fusion.11 = f32[1,8,8,256]{3,2,1,0:T(8,128)S(1)} fusion(pred[8,8,256]{2,1,0:T(8,128)(4,1)S(1)} %copy-done.40, pred[8,8,256]{2,1,0:T(8,128)(4,1)S(1)} %copy-done.39, pred[8,8,256]{2,1,0:T(8,128)(4,1)S(1)} %copy-done.38, pred[8,8,256]{2,1,0:T(8,128)(4,1)S(1)} %copy-done.37, pred[8,8,256]{2,1,0:T(8,128)(4,1)S(1)} %copy-done.36, ...), kind=kLoop, calls=%fused_computation.357 | loop fusion | flops 507904 | bytes 327744 | tf_op jit(solution)/shard_map/stack | solution.py:88
  391.2 10.1 %add_bitcast_fusion.12 = f32[1,8,8,256]{3,2,1,0:T(8,128)S(1)} fusion(pred[8,8,256]{2,1,0:T(8,128)(4,1)S(1)} %copy-done.40, pred[8,8,256]{2,1,0:T(8,128)(4,1)S(1)} %copy-done.39, pred[8,8,256]{2,1,0:T(8,128)(4,1)S(1)} %copy-done.38, pred[8,8,256]{2,1,0:T(8,128)(4,1)S(1)} %copy-done.37, pred[8,8,256]{2,1,0:T(8,128)(4,1)S(1)} %copy-done.36, ...), kind=kLoop, calls=%fused_computation.358 | loop fusion | flops 507904 | bytes 327744 | tf_op jit(solution)/shard_map/stack | solution.py:88
  405.6 3.5 collective-permute-done.32
  409.2 3.0 collective-permute-done.31
  412.6 7.0 %collective-permute-start.34 = (f32[3,1,8,256]{3,2,1,0:T(8,128)S(1)}, f32[3,1,8,256]{3,2,1,0:T(8,128)S(1)}, u32[]{:S(2)}, u32[]{:S(2)}) collective-permute-start(f32[3,1,8,256]{3,2,1,0:T(8,128)S(1)} %slice.2433), channel_id=1, source_target_pairs={{0,16},{16,32},{32,48},{48,64},{64,80},{80,96},{96,112},{112,128},... | collective-permute-start | bytes 73736 | tf_op jit(solution)/shard_map/ppermute | solution.py:16
  419.6 2.4 collective-permute-start.33
  422.1 3.9 collective-permute-done.33
  429.1 10.1 %add_bitcast_fusion.8 = f32[1,8,8,256]{3,2,1,0:T(8,128)S(1)} fusion(pred[8,8,256]{2,1,0:T(8,128)(4,1)S(1)} %copy-done.8, pred[8,8,256]{2,1,0:T(8,128)(4,1)S(1)} %copy-done.7, pred[8,8,256]{2,1,0:T(8,128)(4,1)S(1)} %copy-done.6, pred[8,8,256]{2,1,0:T(8,128)(4,1)S(1)} %copy-done.5, pred[8,8,256]{2,1,0:T(8,128)(4,1)S(1)} %copy-done.4, ...), kind=kLoop, calls=%fused_computation.354 | loop fusion | flops 507904 | bytes 327744 | tf_op jit(solution)/shard_map/stack | solution.py:88
  439.2 10.1 %add_bitcast_fusion.9 = f32[1,8,8,256]{3,2,1,0:T(8,128)S(1)} fusion(pred[8,8,256]{2,1,0:T(8,128)(4,1)S(1)} %copy-done.8, pred[8,8,256]{2,1,0:T(8,128)(4,1)S(1)} %copy-done.7, pred[8,8,256]{2,1,0:T(8,128)(4,1)S(1)} %copy-done.6, pred[8,8,256]{2,1,0:T(8,128)(4,1)S(1)} %copy-done.5, pred[8,8,256]{2,1,0:T(8,128)(4,1)S(1)} %copy-done.4, ...), kind=kLoop, calls=%fused_computation.355 | loop fusion | flops 507904 | bytes 327744 | tf_op jit(solution)/shard_map/stack | solution.py:88
  453.6 3.5 collective-permute-done.37
  457.2 3.0 collective-permute-done.36
  460.6 7.0 %collective-permute-start.39 = (f32[3,1,8,256]{3,2,1,0:T(8,128)S(1)}, f32[3,1,8,256]{3,2,1,0:T(8,128)S(1)}, u32[]{:S(2)}, u32[]{:S(2)}) collective-permute-start(f32[3,1,8,256]{3,2,1,0:T(8,128)S(1)} %slice.2473), channel_id=1, source_target_pairs={{0,16},{16,32},{32,48},{48,64},{64,80},{80,96},{96,112},{112,128},... | collective-permute-start | bytes 73736 | tf_op jit(solution)/shard_map/ppermute | solution.py:16
  467.6 2.4 collective-permute-start.38
  470.1 3.9 collective-permute-done.38
  (354 shorter events, 65.5 us)
Async XLA Ops:
  0.6 7.9 %copy-start.41 = (s32[16,8,256]{2,1,0:T(8,128)S(1)}, s32[16,8,256]{2,1,0:T(8,128)}, u32[]{:S(2)}) copy-start(s32[16,8,256]{2,1,0:T(8,128)} %param.10) | copy-start | bytes 393220
  39.6 6.3 %copy-start.1 = (s32[32,8,256]{2,1,0:T(8,128)S(1)}, s32[32,8,256]{2,1,0:T(8,128)}, u32[]{:S(2)}) copy-start(s32[32,8,256]{2,1,0:T(8,128)} %param.11) | copy-start | bytes 786436
  39.7 37.5 %collective-permute-start = (f32[9,8,8,256]{3,2,1,0:T(8,128)S(1)}, f32[9,8,8,256]{3,2,1,0:T(8,128)S(1)}, u32[]{:S(2)}, u32[]{:S(2)}) collective-permute-start(f32[9,8,8,256]{3,2,1,0:T(8,128)S(1)} %get-tuple-element.272), channel_id=1, source_target_pairs={{16,0},{32,16},{48,32},{64,48},{80,64},{96,80},{112,96},{128,112},... | collective-permute-start | bytes 1769480 | tf_op jit(solution)/shard_map/ppermute | solution.py:16
  77.6 7.3 %collective-permute-start.2 = (f32[3,1,8,256]{3,2,1,0:T(8,128)S(1)}, f32[3,1,8,256]{3,2,1,0:T(8,128)S(1)}, u32[]{:S(2)}, u32[]{:S(2)}) collective-permute-start(f32[3,1,8,256]{3,2,1,0:T(8,128)S(1)} %slice.2180), channel_id=1, source_target_pairs={{16,0},{32,16},{48,32},{64,48},{80,64},{96,80},{112,96},{128,112},... | collective-permute-start | bytes 73736 | tf_op jit(solution)/shard_map/ppermute | solution.py:16
  79.9 8.4 %collective-permute-start.1 = (f32[3,16,1,256]{3,2,1,0:T(1,128)S(1)}, f32[3,16,1,256]{3,2,1,0:T(1,128)S(1)}, u32[]{:S(2)}, u32[]{:S(2)}) collective-permute-start(f32[3,16,1,256]{3,2,1,0:T(1,128)S(1)} %slice.2177), channel_id=1, source_target_pairs={{1,0},{2,1},{3,2},{4,3},{5,4},{6,5},{7,6},{8,7},{9,8},{10,9},{11,1... | collective-permute-start | bytes 147464 | tf_op jit(solution)/shard_map/ppermute | solution.py:16
  88.8 9.2 %collective-permute-start.4 = (f32[3,1,8,256]{3,2,1,0:T(8,128)S(1)}, f32[3,1,8,256]{3,2,1,0:T(8,128)S(1)}, u32[]{:S(2)}, u32[]{:S(2)}) collective-permute-start(f32[3,1,8,256]{3,2,1,0:T(8,128)S(1)} %slice.2193), channel_id=1, source_target_pairs={{0,16},{16,32},{32,48},{48,64},{64,80},{80,96},{96,112},{112,128},... | collective-permute-start | bytes 73736 | tf_op jit(solution)/shard_map/ppermute | solution.py:16
  95.6 6.3 %collective-permute-start.3 = (f32[3,16,1,256]{3,2,1,0:T(1,128)S(1)}, f32[3,16,1,256]{3,2,1,0:T(1,128)S(1)}, u32[]{:S(2)}, u32[]{:S(2)}) collective-permute-start(f32[3,16,1,256]{3,2,1,0:T(1,128)S(1)} %slice.2189), channel_id=1, source_target_pairs={{0,1},{1,2},{2,3},{3,4},{4,5},{5,6},{6,7},{7,8},{8,9},{9,10},{10,1... | collective-permute-start | bytes 147464 | tf_op jit(solution)/shard_map/ppermute | solution.py:16
  102.4 36.3 %collective-permute-start.5 = (f32[9,8,8,256]{3,2,1,0:T(8,128)S(1)}, f32[9,8,8,256]{3,2,1,0:T(8,128)S(1)}, u32[]{:S(2)}, u32[]{:S(2)}) collective-permute-start(f32[9,8,8,256]{3,2,1,0:T(8,128)S(1)} %get-tuple-element.259), channel_id=1, source_target_pairs={{16,0},{32,16},{48,32},{64,48},{80,64},{96,80},{112,96},{128,112},... | collective-permute-start | bytes 1769480 | tf_op jit(solution)/shard_map/ppermute | solution.py:16
  139.1 7.3 %collective-permute-start.7 = (f32[3,1,8,256]{3,2,1,0:T(8,128)S(1)}, f32[3,1,8,256]{3,2,1,0:T(8,128)S(1)}, u32[]{:S(2)}, u32[]{:S(2)}) collective-permute-start(f32[3,1,8,256]{3,2,1,0:T(8,128)S(1)} %slice.2220), channel_id=1, source_target_pairs={{16,0},{32,16},{48,32},{64,48},{80,64},{96,80},{112,96},{128,112},... | collective-permute-start | bytes 73736 | tf_op jit(solution)/shard_map/ppermute | solution.py:16
  141.2 8.4 %collective-permute-start.6 = (f32[3,16,1,256]{3,2,1,0:T(1,128)S(1)}, f32[3,16,1,256]{3,2,1,0:T(1,128)S(1)}, u32[]{:S(2)}, u32[]{:S(2)}) collective-permute-start(f32[3,16,1,256]{3,2,1,0:T(1,128)S(1)} %slice.2217), channel_id=1, source_target_pairs={{1,0},{2,1},{3,2},{4,3},{5,4},{6,5},{7,6},{8,7},{9,8},{10,9},{11,1... | collective-permute-start | bytes 147464 | tf_op jit(solution)/shard_map/ppermute | solution.py:16
  150.1 9.5 %collective-permute-start.9 = (f32[3,1,8,256]{3,2,1,0:T(8,128)S(1)}, f32[3,1,8,256]{3,2,1,0:T(8,128)S(1)}, u32[]{:S(2)}, u32[]{:S(2)}) collective-permute-start(f32[3,1,8,256]{3,2,1,0:T(8,128)S(1)} %slice.2233), channel_id=1, source_target_pairs={{0,16},{16,32},{32,48},{48,64},{64,80},{80,96},{96,112},{112,128},... | collective-permute-start | bytes 73736 | tf_op jit(solution)/shard_map/ppermute | solution.py:16
  157.2 6.3 %collective-permute-start.8 = (f32[3,16,1,256]{3,2,1,0:T(1,128)S(1)}, f32[3,16,1,256]{3,2,1,0:T(1,128)S(1)}, u32[]{:S(2)}, u32[]{:S(2)}) collective-permute-start(f32[3,16,1,256]{3,2,1,0:T(1,128)S(1)} %slice.2229), channel_id=1, source_target_pairs={{0,1},{1,2},{2,3},{3,4},{4,5},{5,6},{6,7},{7,8},{8,9},{9,10},{10,1... | collective-permute-start | bytes 147464 | tf_op jit(solution)/shard_map/ppermute | solution.py:16
  164.0 33.9 %collective-permute-start.10 = (f32[9,8,8,256]{3,2,1,0:T(8,128)S(1)}, f32[9,8,8,256]{3,2,1,0:T(8,128)S(1)}, u32[]{:S(2)}, u32[]{:S(2)}) collective-permute-start(f32[9,8,8,256]{3,2,1,0:T(8,128)S(1)} %get-tuple-element.246), channel_id=1, source_target_pairs={{16,0},{32,16},{48,32},{64,48},{80,64},{96,80},{112,96},{128,112},... | collective-permute-start | bytes 1769480 | tf_op jit(solution)/shard_map/ppermute | solution.py:16
  198.3 7.5 %collective-permute-start.12 = (f32[3,1,8,256]{3,2,1,0:T(8,128)S(1)}, f32[3,1,8,256]{3,2,1,0:T(8,128)S(1)}, u32[]{:S(2)}, u32[]{:S(2)}) collective-permute-start(f32[3,1,8,256]{3,2,1,0:T(8,128)S(1)} %slice.2260), channel_id=1, source_target_pairs={{16,0},{32,16},{48,32},{64,48},{80,64},{96,80},{112,96},{128,112},... | collective-permute-start | bytes 73736 | tf_op jit(solution)/shard_map/ppermute | solution.py:16
  200.4 8.4 %collective-permute-start.11 = (f32[3,16,1,256]{3,2,1,0:T(1,128)S(1)}, f32[3,16,1,256]{3,2,1,0:T(1,128)S(1)}, u32[]{:S(2)}, u32[]{:S(2)}) collective-permute-start(f32[3,16,1,256]{3,2,1,0:T(1,128)S(1)} %slice.2257), channel_id=1, source_target_pairs={{1,0},{2,1},{3,2},{4,3},{5,4},{6,5},{7,6},{8,7},{9,8},{10,9},{11,1... | collective-permute-start | bytes 147464 | tf_op jit(solution)/shard_map/ppermute | solution.py:16
  209.3 9.5 %collective-permute-start.14 = (f32[3,1,8,256]{3,2,1,0:T(8,128)S(1)}, f32[3,1,8,256]{3,2,1,0:T(8,128)S(1)}, u32[]{:S(2)}, u32[]{:S(2)}) collective-permute-start(f32[3,1,8,256]{3,2,1,0:T(8,128)S(1)} %slice.2273), channel_id=1, source_target_pairs={{0,16},{16,32},{32,48},{48,64},{64,80},{80,96},{96,112},{112,128},... | collective-permute-start | bytes 73736 | tf_op jit(solution)/shard_map/ppermute | solution.py:16
  216.3 6.3 %collective-permute-start.13 = (f32[3,16,1,256]{3,2,1,0:T(1,128)S(1)}, f32[3,16,1,256]{3,2,1,0:T(1,128)S(1)}, u32[]{:S(2)}, u32[]{:S(2)}) collective-permute-start(f32[3,16,1,256]{3,2,1,0:T(1,128)S(1)} %slice.2269), channel_id=1, source_target_pairs={{0,1},{1,2},{2,3},{3,4},{4,5},{5,6},{6,7},{7,8},{8,9},{9,10},{10,1... | collective-permute-start | bytes 147464 | tf_op jit(solution)/shard_map/ppermute | solution.py:16
  223.2 33.5 %collective-permute-start.15 = (f32[9,8,8,256]{3,2,1,0:T(8,128)S(1)}, f32[9,8,8,256]{3,2,1,0:T(8,128)S(1)}, u32[]{:S(2)}, u32[]{:S(2)}) collective-permute-start(f32[9,8,8,256]{3,2,1,0:T(8,128)S(1)} %get-tuple-element.233), channel_id=1, source_target_pairs={{16,0},{32,16},{48,32},{64,48},{80,64},{96,80},{112,96},{128,112},... | collective-permute-start | bytes 1769480 | tf_op jit(solution)/shard_map/ppermute | solution.py:16
  257.1 7.5 %collective-permute-start.17 = (f32[3,1,8,256]{3,2,1,0:T(8,128)S(1)}, f32[3,1,8,256]{3,2,1,0:T(8,128)S(1)}, u32[]{:S(2)}, u32[]{:S(2)}) collective-permute-start(f32[3,1,8,256]{3,2,1,0:T(8,128)S(1)} %slice.2300), channel_id=1, source_target_pairs={{16,0},{32,16},{48,32},{64,48},{80,64},{96,80},{112,96},{128,112},... | collective-permute-start | bytes 73736 | tf_op jit(solution)/shard_map/ppermute | solution.py:16
  259.2 8.4 %collective-permute-start.16 = (f32[3,16,1,256]{3,2,1,0:T(1,128)S(1)}, f32[3,16,1,256]{3,2,1,0:T(1,128)S(1)}, u32[]{:S(2)}, u32[]{:S(2)}) collective-permute-start(f32[3,16,1,256]{3,2,1,0:T(1,128)S(1)} %slice.2297), channel_id=1, source_target_pairs={{1,0},{2,1},{3,2},{4,3},{5,4},{6,5},{7,6},{8,7},{9,8},{10,9},{11,1... | collective-permute-start | bytes 147464 | tf_op jit(solution)/shard_map/ppermute | solution.py:16
  268.1 9.5 %collective-permute-start.19 = (f32[3,1,8,256]{3,2,1,0:T(8,128)S(1)}, f32[3,1,8,256]{3,2,1,0:T(8,128)S(1)}, u32[]{:S(2)}, u32[]{:S(2)}) collective-permute-start(f32[3,1,8,256]{3,2,1,0:T(8,128)S(1)} %slice.2313), channel_id=1, source_target_pairs={{0,16},{16,32},{32,48},{48,64},{64,80},{80,96},{96,112},{112,128},... | collective-permute-start | bytes 73736 | tf_op jit(solution)/shard_map/ppermute | solution.py:16
  275.1 6.3 %collective-permute-start.18 = (f32[3,16,1,256]{3,2,1,0:T(1,128)S(1)}, f32[3,16,1,256]{3,2,1,0:T(1,128)S(1)}, u32[]{:S(2)}, u32[]{:S(2)}) collective-permute-start(f32[3,16,1,256]{3,2,1,0:T(1,128)S(1)} %slice.2309), channel_id=1, source_target_pairs={{0,1},{1,2},{2,3},{3,4},{4,5},{5,6},{6,7},{7,8},{8,9},{9,10},{10,1... | collective-permute-start | bytes 147464 | tf_op jit(solution)/shard_map/ppermute | solution.py:16
  281.9 2.8 copy-start.9
  281.9 2.8 copy-start.10
  281.9 2.8 copy-start.11
  282.0 2.8 copy-start.12
  282.0 2.8 copy-start.13
  282.0 2.8 copy-start.14
  282.0 2.8 copy-start.15
  282.0 2.8 copy-start.16
  282.0 2.8 copy-start.17
  282.0 2.8 copy-start.18
  282.0 2.8 copy-start.19
  282.0 2.8 copy-start.20
  282.0 2.8 copy-start.21
  282.1 2.8 copy-start.22
  282.1 2.8 copy-start.23
  282.1 2.8 copy-start.24
  282.2 22.9 %collective-permute-start.20 = (f32[9,8,8,256]{3,2,1,0:T(8,128)S(1)}, f32[9,8,8,256]{3,2,1,0:T(8,128)S(1)}, u32[]{:S(2)}, u32[]{:S(2)}) collective-permute-start(f32[9,8,8,256]{3,2,1,0:T(8,128)S(1)} %get-tuple-element.220), channel_id=1, source_target_pairs={{16,0},{32,16},{48,32},{64,48},{80,64},{96,80},{112,96},{128,112},... | collective-permute-start | bytes 1769480 | tf_op jit(solution)/shard_map/ppermute | solution.py:16
  305.4 7.5 %collective-permute-start.22 = (f32[3,1,8,256]{3,2,1,0:T(8,128)S(1)}, f32[3,1,8,256]{3,2,1,0:T(8,128)S(1)}, u32[]{:S(2)}, u32[]{:S(2)}) collective-permute-start(f32[3,1,8,256]{3,2,1,0:T(8,128)S(1)} %slice.2340), channel_id=1, source_target_pairs={{16,0},{32,16},{48,32},{64,48},{80,64},{96,80},{112,96},{128,112},... | collective-permute-start | bytes 73736 | tf_op jit(solution)/shard_map/ppermute | solution.py:16
  307.5 8.4 %collective-permute-start.21 = (f32[3,16,1,256]{3,2,1,0:T(1,128)S(1)}, f32[3,16,1,256]{3,2,1,0:T(1,128)S(1)}, u32[]{:S(2)}, u32[]{:S(2)}) collective-permute-start(f32[3,16,1,256]{3,2,1,0:T(1,128)S(1)} %slice.2337), channel_id=1, source_target_pairs={{1,0},{2,1},{3,2},{4,3},{5,4},{6,5},{7,6},{8,7},{9,8},{10,9},{11,1... | collective-permute-start | bytes 147464 | tf_op jit(solution)/shard_map/ppermute | solution.py:16
  316.3 9.5 %collective-permute-start.24 = (f32[3,1,8,256]{3,2,1,0:T(8,128)S(1)}, f32[3,1,8,256]{3,2,1,0:T(8,128)S(1)}, u32[]{:S(2)}, u32[]{:S(2)}) collective-permute-start(f32[3,1,8,256]{3,2,1,0:T(8,128)S(1)} %slice.2353), channel_id=1, source_target_pairs={{0,16},{16,32},{32,48},{48,64},{64,80},{80,96},{96,112},{112,128},... | collective-permute-start | bytes 73736 | tf_op jit(solution)/shard_map/ppermute | solution.py:16
  323.4 6.3 %collective-permute-start.23 = (f32[3,16,1,256]{3,2,1,0:T(1,128)S(1)}, f32[3,16,1,256]{3,2,1,0:T(1,128)S(1)}, u32[]{:S(2)}, u32[]{:S(2)}) collective-permute-start(f32[3,16,1,256]{3,2,1,0:T(1,128)S(1)} %slice.2349), channel_id=1, source_target_pairs={{0,1},{1,2},{2,3},{3,4},{4,5},{5,6},{6,7},{7,8},{8,9},{9,10},{10,1... | collective-permute-start | bytes 147464 | tf_op jit(solution)/shard_map/ppermute | solution.py:16
  330.3 22.7 %collective-permute-start.25 = (f32[9,8,8,256]{3,2,1,0:T(8,128)S(1)}, f32[9,8,8,256]{3,2,1,0:T(8,128)S(1)}, u32[]{:S(2)}, u32[]{:S(2)}) collective-permute-start(f32[9,8,8,256]{3,2,1,0:T(8,128)S(1)} %get-tuple-element.207), channel_id=1, source_target_pairs={{16,0},{32,16},{48,32},{64,48},{80,64},{96,80},{112,96},{128,112},... | collective-permute-start | bytes 1769480 | tf_op jit(solution)/shard_map/ppermute | solution.py:16
  353.4 7.5 %collective-permute-start.27 = (f32[3,1,8,256]{3,2,1,0:T(8,128)S(1)}, f32[3,1,8,256]{3,2,1,0:T(8,128)S(1)}, u32[]{:S(2)}, u32[]{:S(2)}) collective-permute-start(f32[3,1,8,256]{3,2,1,0:T(8,128)S(1)} %slice.2380), channel_id=1, source_target_pairs={{16,0},{32,16},{48,32},{64,48},{80,64},{96,80},{112,96},{128,112},... | collective-permute-start | bytes 73736 | tf_op jit(solution)/shard_map/ppermute | solution.py:16
  355.4 8.4 %collective-permute-start.26 = (f32[3,16,1,256]{3,2,1,0:T(1,128)S(1)}, f32[3,16,1,256]{3,2,1,0:T(1,128)S(1)}, u32[]{:S(2)}, u32[]{:S(2)}) collective-permute-start(f32[3,16,1,256]{3,2,1,0:T(1,128)S(1)} %slice.2377), channel_id=1, source_target_pairs={{1,0},{2,1},{3,2},{4,3},{5,4},{6,5},{7,6},{8,7},{9,8},{10,9},{11,1... | collective-permute-start | bytes 147464 | tf_op jit(solution)/shard_map/ppermute | solution.py:16
  364.3 9.5 %collective-permute-start.29 = (f32[3,1,8,256]{3,2,1,0:T(8,128)S(1)}, f32[3,1,8,256]{3,2,1,0:T(8,128)S(1)}, u32[]{:S(2)}, u32[]{:S(2)}) collective-permute-start(f32[3,1,8,256]{3,2,1,0:T(8,128)S(1)} %slice.2393), channel_id=1, source_target_pairs={{0,16},{16,32},{32,48},{48,64},{64,80},{80,96},{96,112},{112,128},... | collective-permute-start | bytes 73736 | tf_op jit(solution)/shard_map/ppermute | solution.py:16
  371.4 6.3 %collective-permute-start.28 = (f32[3,16,1,256]{3,2,1,0:T(1,128)S(1)}, f32[3,16,1,256]{3,2,1,0:T(1,128)S(1)}, u32[]{:S(2)}, u32[]{:S(2)}) collective-permute-start(f32[3,16,1,256]{3,2,1,0:T(1,128)S(1)} %slice.2389), channel_id=1, source_target_pairs={{0,1},{1,2},{2,3},{3,4},{4,5},{5,6},{6,7},{7,8},{8,9},{9,10},{10,1... | collective-permute-start | bytes 147464 | tf_op jit(solution)/shard_map/ppermute | solution.py:16
  378.2 2.8 copy-start.25
  378.2 2.8 copy-start.26
  378.2 2.8 copy-start.27
  378.2 2.8 copy-start.28
  378.2 2.8 copy-start.29
  378.4 22.8 %collective-permute-start.30 = (f32[9,8,8,256]{3,2,1,0:T(8,128)S(1)}, f32[9,8,8,256]{3,2,1,0:T(8,128)S(1)}, u32[]{:S(2)}, u32[]{:S(2)}) collective-permute-start(f32[9,8,8,256]{3,2,1,0:T(8,128)S(1)} %get-tuple-element.194), channel_id=1, source_target_pairs={{16,0},{32,16},{48,32},{64,48},{80,64},{96,80},{112,96},{128,112},... | collective-permute-start | bytes 1769480 | tf_op jit(solution)/shard_map/ppermute | solution.py:16
  401.6 7.5 %collective-permute-start.32 = (f32[3,1,8,256]{3,2,1,0:T(8,128)S(1)}, f32[3,1,8,256]{3,2,1,0:T(8,128)S(1)}, u32[]{:S(2)}, u32[]{:S(2)}) collective-permute-start(f32[3,1,8,256]{3,2,1,0:T(8,128)S(1)} %slice.2420), channel_id=1, source_target_pairs={{16,0},{32,16},{48,32},{64,48},{80,64},{96,80},{112,96},{128,112},... | collective-permute-start | bytes 73736 | tf_op jit(solution)/shard_map/ppermute | solution.py:16
  403.7 8.4 %collective-permute-start.31 = (f32[3,16,1,256]{3,2,1,0:T(1,128)S(1)}, f32[3,16,1,256]{3,2,1,0:T(1,128)S(1)}, u32[]{:S(2)}, u32[]{:S(2)}) collective-permute-start(f32[3,16,1,256]{3,2,1,0:T(1,128)S(1)} %slice.2417), channel_id=1, source_target_pairs={{1,0},{2,1},{3,2},{4,3},{5,4},{6,5},{7,6},{8,7},{9,8},{10,9},{11,1... | collective-permute-start | bytes 147464 | tf_op jit(solution)/shard_map/ppermute | solution.py:16
  412.6 9.5 %collective-permute-start.34 = (f32[3,1,8,256]{3,2,1,0:T(8,128)S(1)}, f32[3,1,8,256]{3,2,1,0:T(8,128)S(1)}, u32[]{:S(2)}, u32[]{:S(2)}) collective-permute-start(f32[3,1,8,256]{3,2,1,0:T(8,128)S(1)} %slice.2433), channel_id=1, source_target_pairs={{0,16},{16,32},{32,48},{48,64},{64,80},{80,96},{96,112},{112,128},... | collective-permute-start | bytes 73736 | tf_op jit(solution)/shard_map/ppermute | solution.py:16
  419.6 6.3 %collective-permute-start.33 = (f32[3,16,1,256]{3,2,1,0:T(1,128)S(1)}, f32[3,16,1,256]{3,2,1,0:T(1,128)S(1)}, u32[]{:S(2)}, u32[]{:S(2)}) collective-permute-start(f32[3,16,1,256]{3,2,1,0:T(1,128)S(1)} %slice.2429), channel_id=1, source_target_pairs={{0,1},{1,2},{2,3},{3,4},{4,5},{5,6},{6,7},{7,8},{8,9},{9,10},{10,1... | collective-permute-start | bytes 147464 | tf_op jit(solution)/shard_map/ppermute | solution.py:16
  426.6 22.7 %collective-permute-start.35 = (f32[9,8,8,256]{3,2,1,0:T(8,128)S(1)}, f32[9,8,8,256]{3,2,1,0:T(8,128)S(1)}, u32[]{:S(2)}, u32[]{:S(2)}) collective-permute-start(f32[9,8,8,256]{3,2,1,0:T(8,128)S(1)} %get-tuple-element.181), channel_id=1, source_target_pairs={{16,0},{32,16},{48,32},{64,48},{80,64},{96,80},{112,96},{128,112},... | collective-permute-start | bytes 1769480 | tf_op jit(solution)/shard_map/ppermute | solution.py:16
  449.6 7.5 %collective-permute-start.37 = (f32[3,1,8,256]{3,2,1,0:T(8,128)S(1)}, f32[3,1,8,256]{3,2,1,0:T(8,128)S(1)}, u32[]{:S(2)}, u32[]{:S(2)}) collective-permute-start(f32[3,1,8,256]{3,2,1,0:T(8,128)S(1)} %slice.2460), channel_id=1, source_target_pairs={{16,0},{32,16},{48,32},{64,48},{80,64},{96,80},{112,96},{128,112},... | collective-permute-start | bytes 73736 | tf_op jit(solution)/shard_map/ppermute | solution.py:16
  451.7 8.4 %collective-permute-start.36 = (f32[3,16,1,256]{3,2,1,0:T(1,128)S(1)}, f32[3,16,1,256]{3,2,1,0:T(1,128)S(1)}, u32[]{:S(2)}, u32[]{:S(2)}) collective-permute-start(f32[3,16,1,256]{3,2,1,0:T(1,128)S(1)} %slice.2457), channel_id=1, source_target_pairs={{1,0},{2,1},{3,2},{4,3},{5,4},{6,5},{7,6},{8,7},{9,8},{10,9},{11,1... | collective-permute-start | bytes 147464 | tf_op jit(solution)/shard_map/ppermute | solution.py:16
  460.5 13.7 %copy-start = (f32[3,16,8,256]{3,2,1,0:T(8,128)}, f32[3,16,8,256]{3,2,1,0:T(8,128)S(1)}, u32[]{:S(2)}) copy-start(f32[3,16,8,256]{3,2,1,0:T(8,128)S(1)} %slice_subtract_fusion) | copy-start | bytes 1179652
  460.6 9.5 %collective-permute-start.39 = (f32[3,1,8,256]{3,2,1,0:T(8,128)S(1)}, f32[3,1,8,256]{3,2,1,0:T(8,128)S(1)}, u32[]{:S(2)}, u32[]{:S(2)}) collective-permute-start(f32[3,1,8,256]{3,2,1,0:T(8,128)S(1)} %slice.2473), channel_id=1, source_target_pairs={{0,16},{16,32},{32,48},{48,64},{64,80},{80,96},{96,112},{112,128},... | collective-permute-start | bytes 73736 | tf_op jit(solution)/shard_map/ppermute | solution.py:16
  467.6 6.3 %collective-permute-start.38 = (f32[3,16,1,256]{3,2,1,0:T(1,128)S(1)}, f32[3,16,1,256]{3,2,1,0:T(1,128)S(1)}, u32[]{:S(2)}, u32[]{:S(2)}) collective-permute-start(f32[3,16,1,256]{3,2,1,0:T(1,128)S(1)} %slice.2469), channel_id=1, source_target_pairs={{0,1},{1,2},{2,3},{3,4},{4,5},{5,6},{6,7},{7,8},{8,9},{9,10},{10,1... | collective-permute-start | bytes 147464 | tf_op jit(solution)/shard_map/ppermute | solution.py:16
  (19 other events, 52.1 us)
where the time goes:
time: 480 us; the launch traced here: 475 us
  other arithmetic  245 us (51%)
  starting transfers between devices  122 us (25%)
  waiting for transfers between devices  83.2 us (17%)
  between operations  12.8 us (3%)
  local copies, waits for them, and re-layouts  12.5 us (3%)
    another operation x20, other arithmetic, lookup(): return jnp.stack(results)  205 us
    ppermute x40, starting transfers between devices, from_behind(): lax.ppermute(value, axis, [(source, source + steps) for source in range(l...  122 us
    ppermute x40, waiting for transfers between devices, from_behind(): lax.ppermute(value, axis, [(source, source + steps) for source in range(l...  83.2 us
    unnamed x2, other arithmetic  20.8 us
    concatenate x8, other arithmetic, body(): stacked = jnp.concatenate([electric, magnetic, coefs], 0)  10.7 us
  transfers between devices with their start and end apart: 40, of which 24 were waited for; matrix products, arithmetic and copies ran while one was open for 44% of the time, Pallas kernels for 0%

commit v1 on v0

v1 whole, which is shorter than its diff:
```python
import jax
import jax.numpy as jnp
from jax import lax
from jax.experimental import pallas as pl
from jax.experimental.pallas import tpu as pltpu
from jax.sharding import PartitionSpec as P

STEPS = 8
SHIFT = 8
HALF = 4
MESH = pl.DeviceIdType.MESH
F32 = jnp.float32


def kernel(
    flags, eps_t, sig_t, ker_t, e_in, h_in, mat, inc,
    o_e, o_h,
    fa, fb, fc, fo, ca, cia, cb, cib, ma, face,
    sm, rm, si, ri, sb1, rb1, xb, rx, sb2, rb2, ss, rs,
):
    nz_dev = lax.axis_size("gz")
    ny_dev = lax.axis_size("gy")
    g = lax.axis_index("gz")
    y = lax.axis_index("gy")
    pz = e_in.shape[1]
    nx = e_in.shape[3]
    slots = nz_dev * pz
    ext = pz + 2 * HALF
    tile = (8, nx)

    def zdev(d):
        return (lax.rem(g + d + nz_dev, nz_dev), y)

    def ydev(d):
        return (g, lax.rem(y + d + ny_dev, ny_dev))

    barrier = pltpu.get_barrier_semaphore()
    partners = [zdev(1), zdev(-1), ydev(1), ydev(-1), zdev(2), zdev(-2)]
    for dev in partners:
        pl.semaphore_signal(barrier, inc=1, device_id=dev, device_id_type=MESH)

    row = lax.broadcasted_iota(jnp.int32, tile, 0)
    lane = lax.broadcasted_iota(jnp.int32, tile, 1)
    low_rows = row < HALF
    first_lane = lane == 0
    last_lane = lane == nx - 1
    at_edge = y == 0
    up_cut = jnp.where((row == HALF - 1) & at_edge, 0.0, 1.0).astype(F32)
    down_cut = jnp.where((row == HALF) & at_edge, 0.0, 1.0).astype(F32)
    face_ok = jnp.where(at_edge, 0.0, 1.0).astype(F32)

    def half_turn(v):
        return pltpu.roll(v, HALF, 0)

    def remote(src, dst, sem_no, dev):
        return pltpu.make_async_remote_copy(
            src, dst, ss.at[sem_no], rs.at[sem_no], device_id=dev, device_id_type=MESH
        )

    for c in range(3):
        fa[c, HALF : HALF + pz] = e_in[c]
        fa[3 + c, HALF : HALF + pz] = h_in[c]
    ma[HALF : HALF + pz] = mat[...]
    for i in range(inc.shape[0] // 2):
        si[i] = jnp.where(low_rows, half_turn(inc[2 * i]), inc[2 * i + 1])

    pl.semaphore_wait(barrier, len(partners))

    top = pl.ds(pz - HALF, HALF)
    bottom = pl.ds(0, HALF)
    lo_halo = pl.ds(0, HALF)
    hi_halo = pl.ds(HALF + pz, HALF)
    first = [
        remote(e_in.at[:, top], fa.at[pl.ds(0, 3), lo_halo], 0, zdev(1)),
        remote(h_in.at[:, top], fa.at[pl.ds(3, 3), lo_halo], 1, zdev(1)),
        remote(mat.at[top], ma.at[lo_halo], 2, zdev(1)),
        remote(e_in.at[:, bottom], fa.at[pl.ds(0, 3), hi_halo], 3, zdev(-1)),
        remote(h_in.at[:, bottom], fa.at[pl.ds(3, 3), hi_halo], 4, zdev(-1)),
        remote(mat.at[bottom], ma.at[hi_halo], 5, zdev(-1)),
    ]
    for copy in first:
        copy.start()
    inc_copy = remote(si, ri, 6, ydev(1))
    inc_copy.start()

    def lookup(ids):
        out = [jnp.zeros(tile, F32) for _ in range(3)]
        for t in range(eps_t.shape[0]):
            here = ids == t
            for i, tab in enumerate((eps_t, sig_t, ker_t)):
                out[i] = jnp.where(here, tab[t], out[i])
        return out[0], 0.5 * out[1], out[2]

    def slot_of(p):
        return lax.rem(g * pz - HALF + p + slots, slots)

    def put(ref, p, values):
        for i in range(3):
            ref[i, p] = values[i]

    def inc_plane(p):
        return lax.rem(slot_of(p), inc.shape[0])

    def own_incoming(p, carry):
        put(cia, p, lookup(inc[inc_plane(p)]))
        return carry

    lax.fori_loop(0, ext, own_incoming, 0)

    for copy in first:
        copy.wait()

    for i in range(ext // 2):
        sm[i] = jnp.where(low_rows, half_turn(ma[2 * i]), ma[2 * i + 1])
    mat_copy = remote(sm, rm, 7, ydev(1))
    mat_copy.start()

    def own_material(p, carry):
        put(ca, p, lookup(ma[p]))
        return carry

    lax.fori_loop(0, ext, own_material, 0)

    counts = []
    total = jnp.int32(0)
    for s in range(STEPS):
        total = total + flags[s]
        counts.append(total)

    def x_up(v):
        return jnp.where(last_lane, 0.0, pltpu.roll(v, nx - 1, 1))

    def x_down(v):
        return jnp.where(first_lane, 0.0, pltpu.roll(v, 1, 1))

    def level(step, k, src, dst, off, coef, coef_inc, inverted, shifted, use_face):
        if inverted:
            h_rows = (row >= HALF - 1 - k) & (row < HALF + k)
            e_rows = (row >= HALF - 1 - k) & (row < HALF + 1 + k)
        else:
            h_rows = (row >= k) & (row < 2 * HALF - 1 - k)
            e_rows = (row >= k + 1) & (row < 2 * HALF - 1 - k)
        count = counts[step]
        cut = count * SHIFT

        def keep(p):
            slot = slot_of(p)
            fresh = (flags[step] == 1) & (slot < cut) & (slot >= cut - SHIFT)
            return jnp.where(fresh, 0.0, 1.0).astype(F32)

        def y_up(v):
            v = pltpu.roll(v, 7, 0)
            return v * up_cut if shifted else v

        def y_down(v, face_no, p):
            v = pltpu.roll(v, 1, 0)
            if shifted:
                v = v * down_cut
            if use_face:
                v = jnp.where(row == 0, face[face_no, p - HALF], v)
            return v

        def magnetic(p):
            stay = keep(p)
            above = jnp.where(slot_of(p) == lax.rem(cut + slots - 1, slots), 0.0, 1.0).astype(F32) * keep(p + 1)
            raw = [src[c, p] for c in range(3)]
            ex, ey, ez = (v * stay for v in raw)
            ux, uy = (src[c, p + 1] * above for c in range(2))
            old = [src[3 + c, p] for c in range(3)]
            hx, hy, hz = (v * stay for v in old)
            hx = hx - 0.5 * ((y_up(ez) - ez) - (uy - ey))
            hy = hy - 0.5 * ((ux - ex) - (x_up(ez) - ez))
            hz = hz - 0.5 * ((x_up(ey) - ey) - (y_up(ex) - ex))
            new = [jnp.where(h_rows, n, o) for n, o in zip((hx, hy, hz), old)]
            return raw, (ex, ey, ez), new

        def store_h(p, new):
            for c in range(3):
                dst[3 + c, p - off] = new[c]

        _, _, new = magnetic(k)
        if dst is src:
            store_h(k, new)

        def plane(p, below):
            raw, e, new = magnetic(p)
            store_h(p, new)
            hx, hy, hz = new
            slot = slot_of(p)
            under = jnp.where(slot == cut, 0.0, 1.0).astype(F32)
            bx, by = (v * under for v in below)
            cx = (hz - y_down(hz, 1, p)) - (hy - by)
            cy = (hx - bx) - (hz - x_down(hz))
            cz = (hy - x_down(hy)) - (hx - y_down(hx, 0, p))
            entered = jnp.full(tile, slot, jnp.int32) < cut
            eps, half_sigma, kerr = (
                jnp.where(entered, coef_inc[i, p], coef[i, p]) for i in range(3)
            )
            permit = eps + kerr * (e[0] * e[0] + e[1] * e[1] + e[2] * e[2])
            inverse = 1.0 / (permit + half_sigma)
            scale = (permit - half_sigma) * inverse
            half_inverse = 0.5 * inverse
            for c, curl in enumerate((cx, cy, cz)):
                updated = scale * e[c] + half_inverse * curl
                dst[c, p - off] = jnp.where(e_rows, updated, raw[c])
            return hx, hy

        lax.fori_loop(k + 1, ext - 1 - k, plane, (new[0], new[1]), unroll=2)

    for k in range(HALF):
        level(k, k, fa, fa, 0, ca, cia, False, False, False)

    def pack_up(p, carry):
        for c in range(3):
            sb1[c, p] = jnp.where(low_rows, half_turn(fa[c, p]), fa[3 + c, p])
        return carry

    lax.fori_loop(0, ext, pack_up, 0)
    for i in range(pz // 4):
        packed = jnp.zeros(tile, F32)
        for j in range(4):
            for n, c in enumerate((0, 2)):
                at = 2 * j + n
                moved = pltpu.roll(fa[3 + c, HALF + 4 * i + j], (at + 8 - (HALF - 1)) % 8, 0)
                packed = jnp.where(row == at, moved, packed)
        xb[i] = packed
    up = [remote(sb1, rb1, 8, ydev(1)), remote(xb, rx, 9, ydev(1))]
    for copy in up:
        copy.start()

    inc_copy.wait()
    mat_copy.wait()

    def joined(low, own):
        return jnp.where(low_rows, low, half_turn(own))

    def shifted_coefs(i, carry):
        pair = rm[i]
        put(cb, 2 * i, lookup(joined(pair, ma[2 * i])))
        put(cb, 2 * i + 1, lookup(joined(half_turn(pair), ma[2 * i + 1])))
        entry = inc_plane(2 * i)
        pair = ri[entry // 2]
        put(cib, 2 * i, lookup(joined(pair, inc[entry])))
        put(cib, 2 * i + 1, lookup(joined(half_turn(pair), inc[entry + 1])))
        return carry

    lax.fori_loop(0, ext // 2, shifted_coefs, 0)
    for copy in up:
        copy.wait()

    def join_up(p, carry):
        for c in range(3):
            got = rb1[c, p]
            fb[c, p] = jnp.where(low_rows, got, half_turn(fa[c, p]))
            fb[3 + c, p] = half_turn(jnp.where(low_rows, fa[3 + c, p], got))
        return carry

    lax.fori_loop(0, ext, join_up, 0)
    for i in range(pz // 4):
        got = rx[i]
        for j in range(4):
            for n in range(2):
                at = 2 * j + n
                face[n, 4 * i + j] = got if at == 0 else pltpu.roll(got, 8 - at, 0)

    for k in range(HALF):
        level(k, k, fb, fb if k < HALF - 1 else fc, 0, cb, cib, True, True, k == HALF - 1)

    edges = [
        remote(fc.at[:, pl.ds(pz, HALF)], fc.at[:, lo_halo], 10, zdev(1)),
        remote(fc.at[:, pl.ds(HALF, HALF)], fc.at[:, hi_halo], 11, zdev(-1)),
    ]
    for copy in edges:
        copy.start()
    for copy in edges:
        copy.wait()

    for k in range(HALF):
        level(HALF + k, k, fc, fc, 0, cb, cib, False, True, False)

    def pack_down(p, carry):
        for c in range(3):
            sb2[c, p] = jnp.where(low_rows, fc[c, p], half_turn(fc[3 + c, p]))
        return carry

    lax.fori_loop(0, ext, pack_down, 0)
    down = remote(sb2, rb2, 12, ydev(-1))
    down.start()
    for n, c in enumerate((0, 2)):
        for p in range(pz):
            face[n, p] = pltpu.roll(fc[3 + c, HALF + p], 8 - (HALF - 1), 0) * face_ok
    down.wait()

    def join_down(p, carry):
        for c in range(3):
            got = rb2[c, p]
            fb[c, p] = half_turn(jnp.where(low_rows, got, fc[c, p]))
            fb[3 + c, p] = jnp.where(low_rows, half_turn(fc[3 + c, p]), got)
        return carry

    lax.fori_loop(0, ext, join_down, 0)

    for k in range(HALF):
        last = k == HALF - 1
        level(HALF + k, k, fb, fo if last else fb, HALF if last else 0, ca, cia, True, False, last)

    result = [
        remote(fo.at[pl.ds(0, 3)], o_e, 13, zdev(-2)),
        remote(fo.at[pl.ds(3, 3)], o_h, 14, zdev(-2)),
    ]
    for copy in result:
        copy.start()
    for copy in result:
        copy.wait()


def body(electric, magnetic, material, incoming, shift_flags, eps_table, sigma_table, kerr_table):
    _, pz, py, nx = electric.shape
    ext = pz + 2 * HALF
    n_inc = incoming.shape[0]
    vmem = pl.BlockSpec(memory_space=pltpu.VMEM)
    smem = pl.BlockSpec(memory_space=pltpu.SMEM)

    def buf(*dims, dtype=F32):
        return pltpu.VMEM((*dims, py, nx), dtype)

    ids = jnp.int32
    return pl.pallas_call(
        kernel,
        out_shape=(
            jax.ShapeDtypeStruct(electric.shape, F32),
            jax.ShapeDtypeStruct(magnetic.shape, F32),
        ),
        in_specs=[smem] * 4 + [vmem] * 4,
        out_specs=(vmem, vmem),
        scratch_shapes=[
            buf(6, ext), buf(6, ext), buf(6, ext), buf(6, pz),
            buf(3, ext), buf(3, ext), buf(3, ext), buf(3, ext),
            buf(ext, dtype=ids), buf(2, pz),
            buf(ext // 2, dtype=ids), buf(ext // 2, dtype=ids),
            buf(n_inc // 2, dtype=ids), buf(n_inc // 2, dtype=ids),
            buf(3, ext), buf(3, ext),
            buf(pz // 4), buf(pz // 4),
            buf(3, ext), buf(3, ext),
            pltpu.SemaphoreType.DMA((15,)),
            pltpu.SemaphoreType.DMA((15,)),
        ],
        compiler_params=pltpu.CompilerParams(
            collective_id=0, has_side_effects=True, vmem_limit_bytes=48 * 1024 * 1024
        ),
        name="window_steps",
    )(shift_flags, eps_table, sigma_table, kerr_table, electric, magnetic, material, incoming)


def solution(mesh):
    return jax.shard_map(
        body,
        mesh=mesh,
        in_specs=(
            P(None, "gz", "gy", None),
            P(None, "gz", "gy", None),
            P("gz", "gy", None),
            P(None, "gy", None),
            P(),
            P(),
            P(),
            P(),
        ),
        out_specs=(P(None, "gz", "gy", None), P(None, "gz", "gy", None)),
        check_vma=False,
    )
```

time: 480 us -> 105 us (0.22)
  the two profiles are of different devices: /device:TPU:119 before, /device:TPU:14 now
where the time goes in v1:
time: 105 us; the launch traced here: 103 us
  Pallas kernels  94.3 us (90%)
  local copies, waits for them, and re-layouts  7.95 us (8%)
    pallas_call x1, Pallas kernels, body(): pl.pallas_call(kernel, out_shape=(jax.ShapeDtypeStruct(electric.shape, F3...  94.3 us
    unnamed x18, local copies, waits for them, and re-layouts  7.95 us

profile of v1, /device:TPU:14, one launch (start us, length us, event | category | flops | bytes accessed | tf_op | source)
XLA Modules:
  0.0 102.9 jit_solution(15555817394229123083)
XLA Ops:
  0.6 0.0 copy-start
  0.6 1.0 copy-done
  1.6 0.0 copy-start.1
  1.6 1.0 copy-done.1
  2.6 0.0 copy-start.2
  2.6 0.9 copy-done.2
  3.6 0.0 copy-start.3
  3.6 0.9 copy-done.3
  4.5 0.0 copy-start.4
  4.5 0.7 copy-done.4
  5.1 0.0 copy-start.5
  5.1 0.7 copy-done.5
  5.8 0.0 copy-start.6
  5.8 0.7 copy-done.6
  6.4 0.0 copy-start.7
  6.5 0.7 copy-done.7
  7.1 94.3 %window_steps.1 = (f32[3,16,8,256]{3,2,1,0:T(8,128)S(1)}, f32[3,16,8,256]{3,2,1,0:T(8,128)S(1)}) custom-call(s32[8]{0:T(128)S(1)} %copy-done.4, f32[16]{0:T(128)S(1)} %copy-done.5, f32[16]{0:T(128)S(1)} %copy-done.6, f32[16]{0:T(128)S(1)} %copy-done.7, f32[3,16,8,256]{3,2,1,0:T(8,128)S(1)} %copy-done, f32[3,16,8,256]{3,2,1,0:T(8,128)S(1)} %copy-done.1, ...), custom_call_target="tpu_custom_call" | custom-call | tf_op jit(solution)/shard_map/window_steps/pallas_call | solution.py:328
  101.4 0.7 copy.12
  102.1 0.7 copy.13
Async XLA Ops:
  0.6 1.0 copy-start
  1.6 1.0 copy-start.1
  2.6 0.9 copy-start.2
  3.6 0.9 copy-start.3
  4.5 0.7 copy-start.4
  5.1 0.7 copy-start.5
  5.8 0.7 copy-start.6
  6.4 0.7 copy-start.7

commit v2 on v1

v2 whole, which is shorter than its diff:
```python
import jax
import jax.numpy as jnp
from jax import lax
from jax.experimental import pallas as pl
from jax.experimental.pallas import tpu as pltpu
from jax.sharding import PartitionSpec as P

STEPS = 8
SHIFT = 8
HALF = 4
MESH = pl.DeviceIdType.MESH
F32 = jnp.float32


def kernel(
    flags, eps_t, sig_t, ker_t, e_in, h_in, mat, inc,
    o_e, o_h,
    fa, fb, fc, fo, ca, cia, cb, cib, ma, face, zs_lo, zs_hi,
    sm, rm, si, ri, sb1, rb1, sb2, rb2, ss, rs,
):
    nz_dev = lax.axis_size("gz")
    ny_dev = lax.axis_size("gy")
    g = lax.axis_index("gz")
    y = lax.axis_index("gy")
    pz = e_in.shape[1]
    nx = e_in.shape[3]
    slots = nz_dev * pz
    ext = pz + 2 * HALF
    tile = (8, nx)
    parts = pz // HALF

    def zdev(d):
        return (lax.rem(g + d + nz_dev, nz_dev), y)

    def ydev(d):
        return (g, lax.rem(y + d + ny_dev, ny_dev))

    barrier = pltpu.get_barrier_semaphore()
    partners = [zdev(1), zdev(-1), ydev(1), ydev(-1), zdev(2), zdev(-2)]
    for dev in partners:
        pl.semaphore_signal(barrier, inc=1, device_id=dev, device_id_type=MESH)

    row = lax.broadcasted_iota(jnp.int32, tile, 0)
    lane = lax.broadcasted_iota(jnp.int32, tile, 1)
    low_rows = row < HALF
    first_lane = lane == 0
    last_lane = lane == nx - 1
    at_edge = y == 0
    up_cut = jnp.where((row == HALF - 1) & at_edge, 0.0, 1.0).astype(F32)
    down_cut = jnp.where((row == HALF) & at_edge, 0.0, 1.0).astype(F32)
    face_ok = jnp.where(at_edge, 0.0, 1.0).astype(F32)

    def half_turn(v):
        return pltpu.roll(v, HALF, 0)

    sem_count = [0]

    def remote(src, dst, dev):
        n = sem_count[0]
        sem_count[0] += 1
        return pltpu.make_async_remote_copy(
            src, dst, ss.at[n], rs.at[n], device_id=dev, device_id_type=MESH
        )

    started = []

    def start(*copies):
        for copy in copies:
            copy.start()
            started.append(copy)

    def loop(lo, hi, step_fn, carry=0, most=6):
        n = hi - lo
        unroll = max(d for d in range(1, most + 1) if n % d == 0)
        return lax.fori_loop(lo, hi, step_fn, carry, unroll=unroll)

    def pack_ids(dst, src, i, j):
        dst[i] = jnp.where(low_rows, half_turn(src[j]), src[j + 1])

    for i in range(pz // 2):
        pack_ids(sm, mat, HALF // 2 + i, 2 * i)
    for i in range(inc.shape[0] // 2):
        pack_ids(si, inc, i, 2 * i)

    pl.semaphore_wait(barrier, len(partners))

    top = pl.ds(pz - HALF, HALF)
    bottom = pl.ds(0, HALF)
    lo_halo = pl.ds(0, HALF)
    hi_halo = pl.ds(HALF + pz, HALF)
    first_lo = [
        remote(e_in.at[:, top], fa.at[pl.ds(0, 3), lo_halo], zdev(1)),
        remote(h_in.at[:, top], fa.at[pl.ds(3, 3), lo_halo], zdev(1)),
        remote(mat.at[top], ma.at[lo_halo], zdev(1)),
    ]
    first_hi = [
        remote(e_in.at[:, bottom], fa.at[pl.ds(0, 3), hi_halo], zdev(-1)),
        remote(h_in.at[:, bottom], fa.at[pl.ds(3, 3), hi_halo], zdev(-1)),
        remote(mat.at[bottom], ma.at[hi_halo], zdev(-1)),
    ]
    start(*first_lo, *first_hi)
    half_ids = HALF // 2
    own_ids = pl.ds(half_ids, pz // 2)
    ids_up = [remote(sm.at[own_ids], rm.at[own_ids], ydev(1)), remote(si, ri, ydev(1))]
    start(*ids_up)

    for c in range(3):
        fa[c, HALF : HALF + pz] = e_in[c]
        fa[3 + c, HALF : HALF + pz] = h_in[c]
    ma[HALF : HALF + pz] = mat[...]

    def lookup(ids):
        out = [jnp.zeros(tile, F32) for _ in range(3)]
        for t in range(eps_t.shape[0]):
            here = ids == t
            for i, tab in enumerate((eps_t, sig_t, ker_t)):
                out[i] = jnp.where(here, tab[t], out[i])
        return out[0], 0.5 * out[1], out[2]

    def slot_of(p):
        return lax.rem(g * pz - HALF + p + slots, slots)

    def put(ref, p, values):
        for i in range(3):
            ref[i, p] = values[i]

    def inc_plane(p):
        return lax.rem(slot_of(p), inc.shape[0])

    def own_incoming(p, carry):
        put(cia, p, lookup(inc[inc_plane(p)]))
        return carry

    def own_material(p, carry):
        put(ca, p, lookup(ma[p]))
        return carry

    loop(HALF, HALF + pz, own_material, most=4)
    loop(0, ext, own_incoming, most=4)

    for copy in first_lo + first_hi:
        copy.wait_recv()
    for i in (0, 1, ext // 2 - 2, ext // 2 - 1):
        pack_ids(sm, ma, i, 2 * i)
    for at in (0, ext // 2 - half_ids):
        ends = pl.ds(at, half_ids)
        ids_up.append(remote(sm.at[ends], rm.at[ends], ydev(1)))
    start(*ids_up[2:])
    loop(0, HALF, own_material, most=4)
    loop(HALF + pz, ext, own_material, most=4)

    counts = []
    total = jnp.int32(0)
    for s in range(STEPS):
        total = total + flags[s]
        counts.append(total)

    def x_up(v):
        return jnp.where(last_lane, 0.0, pltpu.roll(v, nx - 1, 1))

    def x_down(v):
        return jnp.where(first_lane, 0.0, pltpu.roll(v, 1, 1))

    class Level:
        def __init__(self, step, k, src, dst, off, coefs, inverted, shifted):
            self.k, self.src, self.dst, self.off = k, src, dst, off
            self.coef, self.coef_inc = coefs
            self.shifted = shifted
            self.use_face = inverted and k == HALF - 1
            if inverted:
                self.h_rows = (row >= HALF - 1 - k) & (row < HALF + k)
                self.e_rows = (row >= HALF - 1 - k) & (row < HALF + 1 + k)
            else:
                self.h_rows = (row >= k) & (row < 2 * HALF - 1 - k)
                self.e_rows = (row >= k + 1) & (row < 2 * HALF - 1 - k)
            self.flag = flags[step] == 1
            self.cut = counts[step] * SHIFT

        def keep(self, p):
            slot = slot_of(p)
            fresh = self.flag & (slot < self.cut) & (slot >= self.cut - SHIFT)
            return jnp.where(fresh, 0.0, 1.0).astype(F32)

        def y_up(self, v):
            v = pltpu.roll(v, 7, 0)
            return v * up_cut if self.shifted else v

        def y_down(self, v, face_no, p):
            v = pltpu.roll(v, 1, 0)
            if self.shifted:
                v = v * down_cut
            if self.use_face:
                v = jnp.where(row == 0, face[face_no, p - HALF], v)
            return v

        def raw_e(self, p):
            return [self.src[c, p] for c in range(3)]

        def magnetic(self, p, store):
            stay = self.keep(p)
            on_cut = slot_of(p) == lax.rem(self.cut + slots - 1, slots)
            above = jnp.where(on_cut, 0.0, 1.0).astype(F32) * self.keep(p + 1)
            ex, ey, ez = (v * stay for v in self.raw_e(p))
            ux, uy = (self.src[c, p + 1] * above for c in range(2))
            old = [self.src[3 + c, p] for c in range(3)]
            hx, hy, hz = (v * stay for v in old)
            hx = hx - 0.5 * ((self.y_up(ez) - ez) - (uy - ey))
            hy = hy - 0.5 * ((ux - ex) - (x_up(ez) - ez))
            hz = hz - 0.5 * ((x_up(ey) - ey) - (self.y_up(ex) - ex))
            new = [jnp.where(self.h_rows, n, o) for n, o in zip((hx, hy, hz), old)]
            if store:
                for c in range(3):
                    self.dst[3 + c, p - self.off] = new[c]
            return tuple(new)

        def electric(self, p, raw, here, below):
            slot = slot_of(p)
            stay = self.keep(p)
            ex, ey, ez = e = [v * stay for v in raw]
            under = jnp.where(slot == self.cut, 0.0, 1.0).astype(F32)
            hx, hy, hz = here
            bx, by = (v * under for v in below)
            cx = (hz - self.y_down(hz, 1, p)) - (hy - by)
            cy = (hx - bx) - (hz - x_down(hz))
            cz = (hy - x_down(hy)) - (hx - self.y_down(hx, 0, p))
            entered = jnp.full(tile, slot, jnp.int32) < self.cut
            eps, half_sigma, kerr = (
                jnp.where(entered, self.coef_inc[i, p], self.coef[i, p]) for i in range(3)
            )
            permit = eps + kerr * (ex * ex + ey * ey + ez * ez)
            inverse = 1.0 / (permit + half_sigma)
            scale = (permit - half_sigma) * inverse
            half_inverse = 0.5 * inverse
            for c, curl in enumerate((cx, cy, cz)):
                updated = scale * e[c] + half_inverse * curl
                self.dst[c, p - self.off] = jnp.where(self.e_rows, updated, raw[c])

        def upward(self, part):
            k = self.k
            lo = k + 1 if part == 0 else 2 * HALF + 3 + HALF * (part - 1) - k
            hi = 2 * HALF + 3 + HALF * part - k
            if part == 0:
                below = self.magnetic(k, self.dst is self.src)[:2]
            else:
                below = tuple(self.dst[3 + c, lo - 1 - self.off] for c in range(2))

            def plane(p, below):
                raw = self.raw_e(p)
                here = self.magnetic(p, True)
                self.electric(p, raw, here, below)
                return here[:2]

            loop(lo, hi, plane, below)

        def downward(self, part):
            k = self.k
            hi = ext - 2 - k if part == 0 else pz - HALF * part + k
            lo = pz - HALF * (part + 1) + k
            if part == 0:
                above = self.magnetic(hi, True)
            else:
                above = tuple(self.dst[3 + c, hi - self.off] for c in range(3))
            split = part == parts - 1 and self.dst is not self.src

            def plane(p, above, store):
                raw = self.raw_e(p + 1)
                here = self.magnetic(p, store)
                self.electric(p + 1, raw, above, here[:2])
                return here

            end = lo + 1 if split else lo
            above = loop(0, hi - end, lambda i, above: plane(hi - 1 - i, above, True), above)
            if split:
                plane(lo, above, False)

    bounds = [0] + [2 * HALF + HALF * j for j in range(parts - 1)] + [ext]
    up_chunks = [(bounds[j], bounds[j + 1]) for j in range(parts)]
    down_chunks = [(ext - hi, ext - lo) for lo, hi in up_chunks]

    up = []
    at = 0
    levels = [Level(k, k, fa, fa, 0, (ca, cia), False, False) for k in range(HALF)]
    for part, (lo, hi) in enumerate(up_chunks):
        for level in levels:
            level.upward(part)
        base = at

        def pack_up(p, carry):
            for c in range(3):
                sb1[base + 3 * (p - lo) + c] = jnp.where(low_rows, half_turn(fa[c, p]), fa[3 + c, p])
            return carry

        loop(lo, hi, pack_up)
        at += 3 * (hi - lo)
        packed = jnp.zeros(tile, F32)
        for j in range(HALF):
            for n, c in enumerate((0, 2)):
                to = 2 * j + n
                moved = pltpu.roll(fa[3 + c, HALF * (part + 1) + j], (to + 8 - (HALF - 1)) % 8, 0)
                packed = jnp.where(row == to, moved, packed)
        sb1[at] = packed
        at += 1
        span = pl.ds(base, at - base)
        up.append(remote(sb1.at[span], rb1.at[span], ydev(1)))
        start(up[-1])

    for copy in ids_up:
        copy.wait_recv()

    def joined(low, own):
        return jnp.where(low_rows, low, half_turn(own))

    def shifted_coefs(i, carry):
        pair = rm[i]
        put(cb, 2 * i, lookup(joined(pair, ma[2 * i])))
        put(cb, 2 * i + 1, lookup(joined(half_turn(pair), ma[2 * i + 1])))
        entry = inc_plane(2 * i)
        pair = ri[entry // 2]
        put(cib, 2 * i, lookup(joined(pair, inc[entry])))
        put(cib, 2 * i + 1, lookup(joined(half_turn(pair), inc[entry + 1])))
        return carry

    loop(0, ext // 2, shifted_coefs, most=2)

    def join_up(part):
        lo, hi = up_chunks[part]
        base = 3 * lo + part
        up[part].wait_recv()

        def join(p, carry):
            for c in range(3):
                got = rb1[base + 3 * (p - lo) + c]
                fb[c, p] = jnp.where(low_rows, got, half_turn(fa[c, p]))
                fb[3 + c, p] = half_turn(jnp.where(low_rows, fa[3 + c, p], got))
            return carry

        loop(lo, hi, join)
        got = rb1[base + 3 * (hi - lo)]
        for j in range(HALF):
            for n in range(2):
                frm = 2 * j + n
                face[n, HALF * part + j] = got if frm == 0 else pltpu.roll(got, 8 - frm, 0)

    levels = [
        Level(k, k, fb, fb if k < HALF - 1 else fc, 0, (cb, cib), True, True) for k in range(HALF)
    ]
    join_up(0)
    for part in range(parts):
        if part < parts - 1:
            join_up(part + 1)
        for level in levels:
            level.upward(part)
        if part == 0:
            zs_lo[...] = fc[:, HALF : 2 * HALF]
            to_hi = remote(zs_lo, fc.at[:, hi_halo], zdev(-1))
            start(to_hi)
    zs_hi[...] = fc[:, pz : pz + HALF]
    to_lo = remote(zs_hi, fc.at[:, lo_halo], zdev(1))
    start(to_lo)
    to_hi.wait_recv()

    down = []
    levels = [Level(HALF + k, k, fc, fc, 0, (cb, cib), False, True) for k in range(HALF)]
    for part, (lo, hi) in enumerate(down_chunks):
        if part == parts - 1:
            to_lo.wait_recv()
        for level in levels:
            level.downward(part)

        def pack_down(p, carry):
            for c in range(3):
                sb2[3 * p + c] = jnp.where(low_rows, fc[c, p], half_turn(fc[3 + c, p]))
            return carry

        loop(lo, hi, pack_down)
        span = pl.ds(3 * lo, 3 * (hi - lo))
        down.append(remote(sb2.at[span], rb2.at[span], ydev(-1)))
        start(down[-1])

    for p in range(pz):
        for n, c in enumerate((0, 2)):
            face[n, p] = pltpu.roll(fc[3 + c, HALF + p], 8 - (HALF - 1), 0) * face_ok

    def join_down(part):
        lo, hi = down_chunks[part]
        down[part].wait_recv()

        def join(p, carry):
            for c in range(3):
                got = rb2[3 * p + c]
                fb[c, p] = half_turn(jnp.where(low_rows, got, fc[c, p]))
                fb[3 + c, p] = jnp.where(low_rows, half_turn(fc[3 + c, p]), got)
            return carry

        loop(lo, hi, join)

    levels = []
    for k in range(HALF):
        last = k == HALF - 1
        levels.append(Level(HALF + k, k, fb, fo if last else fb, HALF if last else 0, (ca, cia), True, False))
    results = []
    join_down(0)
    for part in range(parts):
        if part < parts - 1:
            join_down(part + 1)
        for level in levels:
            level.downward(part)
        done = pl.ds(pz - HALF * (part + 1), HALF)
        results += [
            remote(fo.at[pl.ds(0, 3), done], o_e.at[:, done], zdev(-2)),
            remote(fo.at[pl.ds(3, 3), done], o_h.at[:, done], zdev(-2)),
        ]
        start(*results[-2:])
    for copy in results:
        copy.wait_recv()
    for copy in started:
        copy.wait_send()


def body(electric, magnetic, material, incoming, shift_flags, eps_table, sigma_table, kerr_table):
    _, pz, py, nx = electric.shape
    ext = pz + 2 * HALF
    n_inc = incoming.shape[0]
    tiles = 3 * ext + pz // HALF
    vmem = pl.BlockSpec(memory_space=pltpu.VMEM)
    smem = pl.BlockSpec(memory_space=pltpu.SMEM)

    def buf(*dims, dtype=F32):
        return pltpu.VMEM((*dims, py, nx), dtype)

    ids = jnp.int32
    return pl.pallas_call(
        kernel,
        out_shape=(
            jax.ShapeDtypeStruct(electric.shape, F32),
            jax.ShapeDtypeStruct(magnetic.shape, F32),
        ),
        in_specs=[smem] * 4 + [vmem] * 4,
        out_specs=(vmem, vmem),
        scratch_shapes=[
            buf(6, ext), buf(6, ext), buf(6, ext), buf(6, pz),
            buf(3, ext), buf(3, ext), buf(3, ext), buf(3, ext),
            buf(ext, dtype=ids), buf(2, pz), buf(6, HALF), buf(6, HALF),
            buf(ext // 2, dtype=ids), buf(ext // 2, dtype=ids),
            buf(n_inc // 2, dtype=ids), buf(n_inc // 2, dtype=ids),
            buf(tiles), buf(tiles), buf(3 * ext), buf(3 * ext),
            pltpu.SemaphoreType.DMA((28,)),
            pltpu.SemaphoreType.DMA((28,)),
        ],
        compiler_params=pltpu.CompilerParams(
            collective_id=0, has_side_effects=True, vmem_limit_bytes=48 * 1024 * 1024
        ),
        name="window_steps",
    )(shift_flags, eps_table, sigma_table, kerr_table, electric, magnetic, material, incoming)


def solution(mesh):
    return jax.shard_map(
        body,
        mesh=mesh,
        in_specs=(
            P(None, "gz", "gy", None),
            P(None, "gz", "gy", None),
            P("gz", "gy", None),
            P(None, "gy", None),
            P(),
            P(),
            P(),
            P(),
        ),
        out_specs=(P(None, "gz", "gy", None), P(None, "gz", "gy", None)),
        check_vma=False,
    )
```

time: 105 us -> 87.1 us (0.83)
  the two profiles are of different devices: /device:TPU:14 before, /device:TPU:4 now
where the time goes in v2:
time: 87.1 us; the launch traced here: 86.9 us
  Pallas kernels  78.3 us (90%)
  local copies, waits for them, and re-layouts  7.95 us (9%)
    pallas_call x1, Pallas kernels, body(): pl.pallas_call(kernel, out_shape=(jax.ShapeDtypeStruct(electric.shape, F3...  78.3 us
    unnamed x18, local copies, waits for them, and re-layouts  7.95 us

profile of v2, /device:TPU:4, one launch (start us, length us, event | category | flops | bytes accessed | tf_op | source)
XLA Modules:
  0.0 86.9 jit_solution(13574340204737357980)
XLA Ops:
  0.6 0.0 copy-start
  0.6 1.0 %copy-done = f32[3,16,8,256]{3,2,1,0:T(8,128)S(1)} copy-done((f32[3,16,8,256]{3,2,1,0:T(8,128)S(1)}, f32[3,16,8,256]{3,2,1,0:T(8,128)}, u32[]{:S(2)}) %copy-start) | copy-done | bytes 393240
  1.6 0.0 copy-start.1
  1.6 1.0 %copy-done.1 = f32[3,16,8,256]{3,2,1,0:T(8,128)S(1)} copy-done((f32[3,16,8,256]{3,2,1,0:T(8,128)S(1)}, f32[3,16,8,256]{3,2,1,0:T(8,128)}, u32[]{:S(2)}) %copy-start.1) | copy-done | bytes 393240
  2.6 0.0 copy-start.2
  2.6 0.9 %copy-done.2 = s32[32,8,256]{2,1,0:T(8,128)S(1)} copy-done((s32[32,8,256]{2,1,0:T(8,128)S(1)}, s32[32,8,256]{2,1,0:T(8,128)}, u32[]{:S(2)}) %copy-start.2) | copy-done | bytes 262168
  3.6 0.0 copy-start.3
  3.6 0.9 %copy-done.3 = s32[16,8,256]{2,1,0:T(8,128)S(1)} copy-done((s32[16,8,256]{2,1,0:T(8,128)S(1)}, s32[16,8,256]{2,1,0:T(8,128)}, u32[]{:S(2)}) %copy-start.3) | copy-done | bytes 131096
  4.5 0.0 copy-start.4
  4.5 0.7 copy-done.4
  5.1 0.0 copy-start.5
  5.1 0.7 copy-done.5
  5.8 0.0 copy-start.6
  5.8 0.7 copy-done.6
  6.4 0.0 copy-start.7
  6.5 0.7 copy-done.7
  7.1 78.3 %window_steps.1 = (f32[3,16,8,256]{3,2,1,0:T(8,128)S(1)}, f32[3,16,8,256]{3,2,1,0:T(8,128)S(1)}) custom-call(s32[8]{0:T(128)S(1)} %copy-done.4, f32[16]{0:T(128)S(1)} %copy-done.5, f32[16]{0:T(128)S(1)} %copy-done.6, f32[16]{0:T(128)S(1)} %copy-done.7, f32[3,16,8,256]{3,2,1,0:T(8,128)S(1)} %copy-done, f32[3,16,8,256]{3,2,1,0:T(8,128)S(1)} %copy-done.1, ...), custom_call_target="tpu_custom_call" | custom-call | tf_op jit(solution)/shard_map/window_steps/pallas_call | solution.py:432
  85.4 0.7 copy.12
  86.1 0.7 copy.13
Async XLA Ops:
  0.6 1.0 %copy-start = (f32[3,16,8,256]{3,2,1,0:T(8,128)S(1)}, f32[3,16,8,256]{3,2,1,0:T(8,128)}, u32[]{:S(2)}) copy-start(f32[3,16,8,256]{3,2,1,0:T(8,128)} %e_in.1) | copy-start | bytes 1179652
  1.6 1.0 %copy-start.1 = (f32[3,16,8,256]{3,2,1,0:T(8,128)S(1)}, f32[3,16,8,256]{3,2,1,0:T(8,128)}, u32[]{:S(2)}) copy-start(f32[3,16,8,256]{3,2,1,0:T(8,128)} %h_in.1) | copy-start | bytes 1179652
  2.6 0.9 %copy-start.2 = (s32[32,8,256]{2,1,0:T(8,128)S(1)}, s32[32,8,256]{2,1,0:T(8,128)}, u32[]{:S(2)}) copy-start(s32[32,8,256]{2,1,0:T(8,128)} %inc.1) | copy-start | bytes 786436
  3.6 0.9 %copy-start.3 = (s32[16,8,256]{2,1,0:T(8,128)S(1)}, s32[16,8,256]{2,1,0:T(8,128)}, u32[]{:S(2)}) copy-start(s32[16,8,256]{2,1,0:T(8,128)} %mat.1) | copy-start | bytes 393220
  4.5 0.7 copy-start.4
  5.1 0.7 copy-start.5
  5.8 0.7 copy-start.6
  6.4 0.7 copy-start.7

commit v3 on v2

--- a/solution.py
+++ b/solution.py
@@ -13,10 +13,10 @@
 
 
 def kernel(
-    flags, eps_t, sig_t, ker_t, e_in, h_in, mat, inc,
+    flags_in, eps_in, sig_in, ker_in, e_in, h_in, mat_in, inc_in,
     o_e, o_h,
-    fa, fb, fc, fo, ca, cia, cb, cib, ma, face, zs_lo, zs_hi,
-    sm, rm, si, ri, sb1, rb1, sb2, rb2, ss, rs,
+    flags, eps_t, sig_t, ker_t, inc, fa, fb, fc, fo, ca, cia, cb, cib, ma, face, zs_lo, zs_hi,
+    sm, rm, si, ri, sb1, rb1, sb2, rb2, ss, rs, ls,
 ):
     nz_dev = lax.axis_size("gz")
     ny_dev = lax.axis_size("gy")
@@ -74,40 +74,47 @@
         unroll = max(d for d in range(1, most + 1) if n % d == 0)
         return lax.fori_loop(lo, hi, step_fn, carry, unroll=unroll)
 
-    def pack_ids(dst, src, i, j):
-        dst[i] = jnp.where(low_rows, half_turn(src[j]), src[j + 1])
-
-    for i in range(pz // 2):
-        pack_ids(sm, mat, HALF // 2 + i, 2 * i)
-    for i in range(inc.shape[0] // 2):
-        pack_ids(si, inc, i, 2 * i)
-
-    pl.semaphore_wait(barrier, len(partners))
+    def pack_ids(dst, src, i):
+        dst[i] = jnp.where(low_rows, half_turn(src[2 * i]), src[2 * i + 1])
 
     top = pl.ds(pz - HALF, HALF)
     bottom = pl.ds(0, HALF)
     lo_halo = pl.ds(0, HALF)
     hi_halo = pl.ds(HALF + pz, HALF)
-    first_lo = [
-        remote(e_in.at[:, top], fa.at[pl.ds(0, 3), lo_halo], zdev(1)),
-        remote(h_in.at[:, top], fa.at[pl.ds(3, 3), lo_halo], zdev(1)),
-        remote(mat.at[top], ma.at[lo_halo], zdev(1)),
+    own = pl.ds(HALF, pz)
+    fields = [(e_in, 0), (h_in, 3)]
+    inputs = [
+        (inc_in, inc),
+        (mat_in, ma.at[own]),
+        (flags_in, flags),
+        (eps_in, eps_t),
+        (sig_in, sig_t),
+        (ker_in, ker_t),
+    ] + [(ref, fa.at[pl.ds(c, 3), own]) for ref, c in fields]
+    inputs = [pltpu.make_async_copy(src, dst, ls.at[i]) for i, (src, dst) in enumerate(inputs)]
+    for copy in inputs:
+        copy.start()
+
+    first_lo = [remote(mat_in.at[top], ma.at[lo_halo], zdev(1))] + [
+        remote(ref.at[:, top], fa.at[pl.ds(c, 3), lo_halo], zdev(1)) for ref, c in fields
     ]
-    first_hi = [
-        remote(e_in.at[:, bottom], fa.at[pl.ds(0, 3), hi_halo], zdev(-1)),
-        remote(h_in.at[:, bottom], fa.at[pl.ds(3, 3), hi_halo], zdev(-1)),
-        remote(mat.at[bottom], ma.at[hi_halo], zdev(-1)),
+    first_hi = [remote(mat_in.at[bottom], ma.at[hi_halo], zdev(-1))] + [
+        remote(ref.at[:, bottom], fa.at[pl.ds(c, 3), hi_halo], zdev(-1)) for ref, c in fields
     ]
+
+    pl.semaphore_wait(barrier, len(partners))
     start(*first_lo, *first_hi)
+
+    for copy in inputs:
+        copy.wait()
     half_ids = HALF // 2
     own_ids = pl.ds(half_ids, pz // 2)
+    for i in range(pz // 2):
+        pack_ids(sm, ma, half_ids + i)
+    for i in range(inc.shape[0] // 2):
+        pack_ids(si, inc, i)
     ids_up = [remote(sm.at[own_ids], rm.at[own_ids], ydev(1)), remote(si, ri, ydev(1))]
     start(*ids_up)
-
-    for c in range(3):
-        fa[c, HALF : HALF + pz] = e_in[c]
-        fa[3 + c, HALF : HALF + pz] = h_in[c]
-    ma[HALF : HALF + pz] = mat[...]
 
     def lookup(ids):
         out = [jnp.zeros(tile, F32) for _ in range(3)]
@@ -138,11 +145,11 @@
     loop(HALF, HALF + pz, own_material, most=4)
     loop(0, ext, own_incoming, most=4)
 
-    for copy in first_lo + first_hi:
+    for copy in first_lo + first_hi[:1]:
         copy.wait_recv()
-    for i in (0, 1, ext // 2 - 2, ext // 2 - 1):
-        pack_ids(sm, ma, i, 2 * i)
     for at in (0, ext // 2 - half_ids):
+        for i in range(half_ids):
+            pack_ids(sm, ma, at + i)
         ends = pl.ds(at, half_ids)
         ids_up.append(remote(sm.at[ends], rm.at[ends], ydev(1)))
     start(*ids_up[2:])
@@ -281,6 +288,9 @@
     at = 0
     levels = [Level(k, k, fa, fa, 0, (ca, cia), False, False) for k in range(HALF)]
     for part, (lo, hi) in enumerate(up_chunks):
+        if part == parts - 1:
+            for copy in first_hi[1:]:
+                copy.wait_recv()
         for level in levels:
             level.upward(part)
         base = at
@@ -398,7 +408,15 @@
     for k in range(HALF):
         last = k == HALF - 1
         levels.append(Level(HALF + k, k, fb, fo if last else fb, HALF if last else 0, (ca, cia), True, False))
+    crossing = lax.rem(g, nz_dev // 2) < 2
     results = []
+
+    def start_results(copies, now):
+        @pl.when(now)
+        def _():
+            for copy in copies:
+                copy.start()
+
     join_down(0)
     for part in range(parts):
         if part < parts - 1:
@@ -410,10 +428,11 @@
             remote(fo.at[pl.ds(0, 3), done], o_e.at[:, done], zdev(-2)),
             remote(fo.at[pl.ds(3, 3), done], o_h.at[:, done], zdev(-2)),
         ]
-        start(*results[-2:])
+        start_results(results[-2:], jnp.logical_not(crossing))
+    start_results(results, crossing)
     for copy in results:
         copy.wait_recv()
-    for copy in started:
+    for copy in started + results:
         copy.wait_send()
 
 
@@ -423,7 +442,6 @@
     n_inc = incoming.shape[0]
     tiles = 3 * ext + pz // HALF
     vmem = pl.BlockSpec(memory_space=pltpu.VMEM)
-    smem = pl.BlockSpec(memory_space=pltpu.SMEM)
 
     def buf(*dims, dtype=F32):
         return pltpu.VMEM((*dims, py, nx), dtype)
@@ -435,20 +453,24 @@
             jax.ShapeDtypeStruct(electric.shape, F32),
             jax.ShapeDtypeStruct(magnetic.shape, F32),
         ),
-        in_specs=[smem] * 4 + [vmem] * 4,
+        in_specs=[pl.BlockSpec(memory_space=pltpu.HBM)] * 8,
         out_specs=(vmem, vmem),
         scratch_shapes=[
+            pltpu.SMEM(shift_flags.shape, ids),
+            *[pltpu.SMEM(t.shape, F32) for t in (eps_table, sigma_table, kerr_table)],
+            buf(n_inc, dtype=ids),
             buf(6, ext), buf(6, ext), buf(6, ext), buf(6, pz),
             buf(3, ext), buf(3, ext), buf(3, ext), buf(3, ext),
             buf(ext, dtype=ids), buf(2, pz), buf(6, HALF), buf(6, HALF),
             buf(ext // 2, dtype=ids), buf(ext // 2, dtype=ids),
             buf(n_inc // 2, dtype=ids), buf(n_inc // 2, dtype=ids),
             buf(tiles), buf(tiles), buf(3 * ext), buf(3 * ext),
-            pltpu.SemaphoreType.DMA((28,)),
-            pltpu.SemaphoreType.DMA((28,)),
+            pltpu.SemaphoreType.DMA((30,)),
+            pltpu.SemaphoreType.DMA((30,)),
+            pltpu.SemaphoreType.DMA((8,)),
         ],
         compiler_params=pltpu.CompilerParams(
-            collective_id=0, has_side_effects=True, vmem_limit_bytes=48 * 1024 * 1024
+            collective_id=0, has_side_effects=True, vmem_limit_bytes=67_000_000
         ),
         name="window_steps",
     )(shift_flags, eps_table, sigma_table, kerr_table, electric, magnetic, material, incoming)

time: 87.1 us -> 74.9 us (0.86)
  the two profiles are of different devices: /device:TPU:4 before, /device:TPU:14 now
where the time goes in v3:
time: 74.9 us; the launch traced here: 74.8 us
  Pallas kernels  71.5 us (95%)
  local copies, waits for them, and re-layouts  2.57 us (3%)
    pallas_call x1, Pallas kernels, body(): pl.pallas_call(kernel, out_shape=(jax.ShapeDtypeStruct(electric.shape, F3...  71.5 us
    unnamed x4, local copies, waits for them, and re-layouts  2.57 us

profile of v3, /device:TPU:14, one launch (start us, length us, event | category | flops | bytes accessed | tf_op | source)
XLA Modules:
  0.0 74.8 jit_solution(3837258671145254962)
XLA Ops:
  0.6 71.5 %window_steps.1 = (f32[3,16,8,256]{3,2,1,0:T(8,128)}, f32[3,16,8,256]{3,2,1,0:T(8,128)}) custom-call(s32[8]{0:T(128)} %flags_in.1, f32[16]{0:T(128)} %eps_in.1, f32[16]{0:T(128)} %sig_in.1, f32[16]{0:T(128)} %ker_in.1, f32[3,16,8,256]{3,2,1,0:T(8,128)} %e_in.1, f32[3,16,8,256]{3,2,1,0:T(8,128)} %h_in.1, s32[16,8,256]{2,1,0:T(8,128)} %mat_in.1, ...), custom_call_target="tpu_custom_call" | custom-call | tf_op jit(solution)/shard_map/window_steps/pallas_call | solution.py:450
  72.2 0.0 copy-start
  72.2 1.8 %copy.12 = f32[3,16,8,256]{3,2,1,0:T(8,128)} copy(f32[3,16,8,256]{3,2,1,0:T(8,128)} %get-tuple-element.4) | data formatting | bytes 786432
  74.0 0.0 copy-done
  74.0 0.7 copy.13
Async XLA Ops:
  72.2 1.8 %copy-start = (f32[3,16,8,256]{3,2,1,0:T(8,128)S(1)}, f32[3,16,8,256]{3,2,1,0:T(8,128)}, u32[]{:S(2)}) copy-start(f32[3,16,8,256]{3,2,1,0:T(8,128)} %get-tuple-element.5) | copy-start | bytes 1179652

commit v4 on v3

--- a/solution.py
+++ b/solution.py
@@ -14,7 +14,7 @@
 
 def kernel(
     flags_in, eps_in, sig_in, ker_in, e_in, h_in, mat_in, inc_in,
-    o_e, o_h,
+    out,
     flags, eps_t, sig_t, ker_t, inc, fa, fb, fc, fo, ca, cia, cb, cib, ma, face, zs_lo, zs_hi,
     sm, rm, si, ri, sb1, rb1, sb2, rb2, ss, rs, ls,
 ):
@@ -425,10 +425,9 @@
             level.downward(part)
         done = pl.ds(pz - HALF * (part + 1), HALF)
         results += [
-            remote(fo.at[pl.ds(0, 3), done], o_e.at[:, done], zdev(-2)),
-            remote(fo.at[pl.ds(3, 3), done], o_h.at[:, done], zdev(-2)),
+            remote(fo.at[:, done], out.at[:, done], zdev(-2)),
         ]
-        start_results(results[-2:], jnp.logical_not(crossing))
+        start_results(results[-1:], jnp.logical_not(crossing))
     start_results(results, crossing)
     for copy in results:
         copy.wait_recv()
@@ -441,20 +440,16 @@
     ext = pz + 2 * HALF
     n_inc = incoming.shape[0]
     tiles = 3 * ext + pz // HALF
-    vmem = pl.BlockSpec(memory_space=pltpu.VMEM)
 
     def buf(*dims, dtype=F32):
         return pltpu.VMEM((*dims, py, nx), dtype)
 
     ids = jnp.int32
-    return pl.pallas_call(
+    fields = pl.pallas_call(
         kernel,
-        out_shape=(
-            jax.ShapeDtypeStruct(electric.shape, F32),
-            jax.ShapeDtypeStruct(magnetic.shape, F32),
-        ),
+        out_shape=jax.ShapeDtypeStruct((6, pz, py, nx), F32),
         in_specs=[pl.BlockSpec(memory_space=pltpu.HBM)] * 8,
-        out_specs=(vmem, vmem),
+        out_specs=pl.BlockSpec(memory_space=pltpu.HBM),
         scratch_shapes=[
             pltpu.SMEM(shift_flags.shape, ids),
             *[pltpu.SMEM(t.shape, F32) for t in (eps_table, sigma_table, kerr_table)],
@@ -474,6 +469,7 @@
         ),
         name="window_steps",
     )(shift_flags, eps_table, sigma_table, kerr_table, electric, magnetic, material, incoming)
+    return fields[:3], fields[3:]
 
 
 def solution(mesh):

time: 74.9 us -> 73.6 us (0.983)
    unnamed x4 -> x0, local copies, waits for them, and re-layouts: 2.57 us -> none
    slice x0 -> x1, local copies, waits for them, and re-layouts: none -> 2.08 us  [body(): return (fields[:3], fields[3:])]
    pallas_call x1, Pallas kernels: 71.5 us -> 70.8 us  [body(): pl.pallas_call(kernel, out_shape=jax.ShapeDtypeStruct((6, pz, py, nx), F3...]
where the time goes in v4:
time: 73.6 us; the launch traced here: 73.5 us
  Pallas kernels  70.8 us (96%)
  local copies, waits for them, and re-layouts  2.08 us (3%)
    pallas_call x1, Pallas kernels, body(): pl.pallas_call(kernel, out_shape=jax.ShapeDtypeStruct((6, pz, py, nx), F3...  70.8 us
    slice x1, local copies, waits for them, and re-layouts, body(): return (fields[:3], fields[3:])  2.08 us

profile of v4, /device:TPU:14, one launch (start us, length us, event | category | flops | bytes accessed | tf_op | source)
XLA Modules:
  0.0 73.5 jit_solution(5974259867761263318)
XLA Ops:
  0.6 70.8 %window_steps.1 = f32[6,16,8,256]{3,2,1,0:T(8,128)} custom-call(s32[8]{0:T(128)} %flags_in.1, f32[16]{0:T(128)} %eps_in.1, f32[16]{0:T(128)} %sig_in.1, f32[16]{0:T(128)} %ker_in.1, f32[3,16,8,256]{3,2,1,0:T(8,128)} %e_in.1, f32[3,16,8,256]{3,2,1,0:T(8,128)} %h_in.1, s32[16,8,256]{2,1,0:T(8,128)} %mat_in.1, s32[32,8,256]{2,1,0:T(8,128)} %inc_in.1), custom_call_target="tpu_custom_call" | custom-call | tf_op jit(solution)/shard_map/window_steps/pallas_call | solution.py:448
  71.4 2.1 %fusion = (f32[3,16,8,256]{3,2,1,0:T(8,128)}, f32[3,16,8,256]{3,2,1,0:T(8,128)}) fusion(f32[6,16,8,256]{3,2,1,0:T(8,128)} %window_steps.1), kind=kLoop, calls=%fused_computation | loop fusion | bytes 1572864 | tf_op jit(solution)/shard_map/slice | solution.py:472

commit v5 on v4

--- a/solution.py
+++ b/solution.py
@@ -280,19 +280,21 @@
             if split:
                 plane(lo, above, False)
 
-    bounds = [0] + [2 * HALF + HALF * j for j in range(parts - 1)] + [ext]
-    up_chunks = [(bounds[j], bounds[j + 1]) for j in range(parts)]
+    bounds = [0] + [HALF * j for j in range(2, parts + 2)] + [ext]
+    up_chunks = [(bounds[j], bounds[j + 1]) for j in range(parts + 1)]
     down_chunks = [(ext - hi, ext - lo) for lo, hi in up_chunks]
+    down_chunks[-2:] = [(0, 2 * HALF)]
 
     up = []
     at = 0
     levels = [Level(k, k, fa, fa, 0, (ca, cia), False, False) for k in range(HALF)]
-    for part, (lo, hi) in enumerate(up_chunks):
-        if part == parts - 1:
+    for chunk, (lo, hi) in enumerate(up_chunks):
+        if chunk == parts - 1:
             for copy in first_hi[1:]:
                 copy.wait_recv()
-        for level in levels:
-            level.upward(part)
+        if chunk < parts:
+            for level in levels:
+                level.upward(chunk)
         base = at
 
         def pack_up(p, carry):
@@ -302,14 +304,15 @@
 
         loop(lo, hi, pack_up)
         at += 3 * (hi - lo)
-        packed = jnp.zeros(tile, F32)
-        for j in range(HALF):
-            for n, c in enumerate((0, 2)):
-                to = 2 * j + n
-                moved = pltpu.roll(fa[3 + c, HALF * (part + 1) + j], (to + 8 - (HALF - 1)) % 8, 0)
-                packed = jnp.where(row == to, moved, packed)
-        sb1[at] = packed
-        at += 1
+        if chunk < parts:
+            packed = jnp.zeros(tile, F32)
+            for j in range(HALF):
+                for n, c in enumerate((0, 2)):
+                    to = 2 * j + n
+                    moved = pltpu.roll(fa[3 + c, HALF * (chunk + 1) + j], (to + 8 - (HALF - 1)) % 8, 0)
+                    packed = jnp.where(row == to, moved, packed)
+            sb1[at] = packed
+            at += 1
         span = pl.ds(base, at - base)
         up.append(remote(sb1.at[span], rb1.at[span], ydev(1)))
         start(up[-1])
@@ -345,6 +348,8 @@
             return carry
 
         loop(lo, hi, join)
+        if part == parts:
+            return
         got = rb1[base + 3 * (hi - lo)]
         for j in range(HALF):
             for n in range(2):
@@ -356,8 +361,7 @@
     ]
     join_up(0)
     for part in range(parts):
-        if part < parts - 1:
-            join_up(part + 1)
+        join_up(part + 1)
         for level in levels:
             level.upward(part)
         if part == 0:
@@ -371,11 +375,12 @@
 
     down = []
     levels = [Level(HALF + k, k, fc, fc, 0, (cb, cib), False, True) for k in range(HALF)]
-    for part, (lo, hi) in enumerate(down_chunks):
-        if part == parts - 1:
+    for chunk, (lo, hi) in enumerate(down_chunks):
+        if chunk == parts - 1:
             to_lo.wait_recv()
-        for level in levels:
-            level.downward(part)
+        if chunk < parts:
+            for level in levels:
+                level.downward(chunk)
 
         def pack_down(p, carry):
             for c in range(3):
@@ -428,8 +433,10 @@
             remote(fo.at[:, done], out.at[:, done], zdev(-2)),
         ]
         start_results(results[-1:], jnp.logical_not(crossing))
+    for copy in results[:2]:
+        copy.wait_recv()
     start_results(results, crossing)
-    for copy in results:
+    for copy in results[2:]:
         copy.wait_recv()
     for copy in started + results:
         copy.wait_send()

time: 73.6 us -> 73.4 us (level)
  no operation moved by 1% of the time
where the time goes in v5:
time: 73.4 us; the launch traced here: 73.3 us
  Pallas kernels  70.6 us (96%)
  local copies, waits for them, and re-layouts  2.08 us (3%)
    pallas_call x1, Pallas kernels, body(): pl.pallas_call(kernel, out_shape=jax.ShapeDtypeStruct((6, pz, py, nx), F3...  70.6 us
    slice x1, local copies, waits for them, and re-layouts, body(): return (fields[:3], fields[3:])  2.08 us

profile of v5, /device:TPU:14, one launch (start us, length us, event | category | flops | bytes accessed | tf_op | source)
XLA Modules:
  0.0 73.3 jit_solution(6963075905215979466)
XLA Ops:
  0.6 70.6 %window_steps.1 = f32[6,16,8,256]{3,2,1,0:T(8,128)} custom-call(s32[8]{0:T(128)} %flags_in.1, f32[16]{0:T(128)} %eps_in.1, f32[16]{0:T(128)} %sig_in.1, f32[16]{0:T(128)} %ker_in.1, f32[3,16,8,256]{3,2,1,0:T(8,128)} %e_in.1, f32[3,16,8,256]{3,2,1,0:T(8,128)} %h_in.1, s32[16,8,256]{2,1,0:T(8,128)} %mat_in.1, s32[32,8,256]{2,1,0:T(8,128)} %inc_in.1), custom_call_target="tpu_custom_call" | custom-call | tf_op jit(solution)/shard_map/window_steps/pallas_call | solution.py:455
  71.2 2.1 %fusion = (f32[3,16,8,256]{3,2,1,0:T(8,128)}, f32[3,16,8,256]{3,2,1,0:T(8,128)}) fusion(f32[6,16,8,256]{3,2,1,0:T(8,128)} %window_steps.1), kind=kLoop, calls=%fused_computation | loop fusion | bytes 1572864 | tf_op jit(solution)/shard_map/slice | solution.py:479
